TPU v7x, 512 devices: a whole 4x4x16 slice. The times are simulated.
512 devices in a mesh: line: 16 (over z), bus: 32 (over x, y, core).
Axes of the slice: x: 4, y: 4, z: 16, core: 2. Of those that a mesh axis runs over, the one named last changes fastest.
Arguments:
- transfer_factors: float32 [4096, 65536], P('line', 'bus'), may hold values from -0.24 to 0.24
- line_flows: float32 [4096], P('line'), may hold values from -6 to 6
- from_bus: int32 [4096], replicated, may hold values from 0 to 65535
- to_bus: int32 [4096], replicated, may hold values from 0 to 65535
- tripped: int32 [2, 64], replicated, may hold values from 0 to 4095, as said below
Outputs:
- new_factors: float32 [4096, 65536], P('line', 'bus')
- new_flows: float32 [4096], P('line')
Inputs may be any that keep to these rules, and one draw needn't show every extreme that they name: No line is tripped twice; in every segment at most 8 tripped lines lie in one aligned block of 256 consecutive lines, and some block holds exactly 8.
All inputs are finite; a program needn't handle non-finite values.
Results may differ from a plain program's by a relative error of at most 0.00018.
Values sent between devices are 32-bit elements; how exact they have to be, the bound alone decides.
A program may use at most 64 MiB of HBM per device.

v0:
```python
import jax
import jax.numpy as jnp
from jax import lax
from jax.sharding import PartitionSpec as P


def chol_solve(factor_lower, right):
    middle = lax.linalg.triangular_solve(factor_lower, right, left_side=True, lower=True)
    return lax.linalg.triangular_solve(
        factor_lower, middle, left_side=True, lower=True, transpose_a=True
    )


def column_select(col_global, from_bus, to_bus, outage_ids):
    from_ids = jnp.take(from_bus, outage_ids)
    to_ids = jnp.take(to_bus, outage_ids)
    return (col_global[:, None] == from_ids[None, :]).astype(jnp.float32) - (
        col_global[:, None] == to_ids[None, :]
    ).astype(jnp.float32)


def per_device(transfer_factors, line_flows, from_bus, to_bus, tripped):
    precise = lax.Precision.HIGHEST
    local_rows, local_cols = transfer_factors.shape
    outages = tripped.shape[1]
    line_index = lax.axis_index("line")
    bus_index = lax.axis_index("bus")
    row_global = line_index * local_rows + jnp.arange(local_rows, dtype=jnp.int32)
    col_global = bus_index * local_cols + jnp.arange(local_cols, dtype=jnp.int32)
    factors = transfer_factors
    flows_now = line_flows
    identity = jnp.eye(outages, dtype=jnp.float32)
    for segment_index in range(tripped.shape[0]):
        outage_ids = tripped[segment_index]
        terminal_select = column_select(col_global, from_bus, to_bus, outage_ids)
        outage_select = (outage_ids[:, None] == row_global[None, :]).astype(jnp.float32)
        terminal_part = jnp.dot(factors, terminal_select, precision=precise)
        terminal = lax.psum(terminal_part, "bus")
        outage_terms = lax.psum(jnp.dot(outage_select, terminal, precision=precise), "line")
        outage_rows, outage_flows = lax.psum(
            (
                jnp.dot(outage_select, factors, precision=precise),
                jnp.dot(outage_select, flows_now, precision=precise),
            ),
            "line",
        )
        capacitance = identity - outage_terms
        factor_lower = jnp.linalg.cholesky(jnp.dot(capacitance, capacitance.T, precision=precise))
        update_weights = chol_solve(
            factor_lower, jnp.dot(capacitance, terminal.T, precision=precise)
        )
        factors = factors + jnp.dot(update_weights.T, outage_rows, precision=precise)
        flows_now = flows_now + jnp.dot(update_weights.T, outage_flows, precision=precise)
        keep_mask = 1.0 - jnp.sum(outage_select, axis=0)
        factors = factors * keep_mask[:, None]
        flows_now = flows_now * keep_mask
    return (factors, flows_now)


def solution(mesh):
    placed = (P("line", "bus"), P("line"), P(), P(), P())
    return jax.shard_map(
        per_device,
        mesh=mesh,
        in_specs=placed,
        out_specs=(P("line", "bus"), P("line")),
        check_vma=False,
    )
```

profile of v0, /device:TPU:6, one launch (start us, length us, event | category | flops | bytes accessed | tf_op | source)
XLA Modules:
  0.0 564.4 jit_solution(1560953369744594784)
XLA Ops:
  7.2 0.0 copy-start
  7.2 0.0 copy-start.3
  7.2 0.0 copy-start.2
  7.2 0.0 all-reduce.7.cloned.1.call-start
  7.3 0.8 compare_select_fusion
  8.1 0.0 copy-done
  8.1 0.8 gather_fusion.1
  8.9 1.5 gather_fusion
  10.4 4.6 convolution_bitcast_fusion
  15.0 0.0 copy-start.1
  15.0 0.0 all-reduce.7.cloned.1.call-update
  15.0 0.0 all-reduce.9.cloned.1.call-start
  15.0 0.0 copy-done.3
  15.1 0.0 copy-done.2
  15.1 0.0 copy-start.4
  15.1 1.7 fusion.25
  16.8 0.0 all-reduce.9.cloned.1.call-update
  16.9 0.0 all-reduce.11.cloned.1.call-start
  16.9 0.8 gather_fusion.3
  17.7 0.0 copy-done.1
  17.7 0.8 gather_fusion.2
  18.5 0.0 copy-done.4
  18.5 0.2 convolution_bitcast_fusion.2
  18.6 0.1 fusion.30
  18.8 126.3 %all-reduce.7.cloned.1.call-done = f32[256,64]{0,1:T(8,128)} async-done(((f32[256,64]{0,1:T(8,128)}), f32[256,64]{0,1:T(8,128)}) %all-reduce.7.cloned.1.call-update) | async-done | bytes 65552 | tf_op jit(solution)/shard_map/psum | solution.py:38
  145.1 1.1 fusion.27
  146.1 57.1 %all-reduce.1 = (f32[64,64]{1,0:T(8,128)S(1)}, f32[64]{0:T(128)S(1)}) all-reduce(f32[64,64]{1,0:T(8,128)S(1)} %fusion.27, f32[64]{0:T(128)S(1)} %convolution_bitcast_fusion.2), channel_id=1, replica_groups=mesh['line'=16,'bus'=32] {'line'}, use_global_device_ids=true, to_apply=%region_1.3 | all-reduce | flops 4160 | bytes 33280 | tf_op jit(solution)/shard_map/psum | solution.py:39
  203.3 0.2 fusion.60
  203.5 0.1 copy.11
  203.5 5.8 %cholesky.44 = f32[64,64]{1,0:T(8,128)S(1)} custom-call(f32[64,64]{1,0:T(8,128)S(1)} %fusion.46), custom_call_target="Cholesky" | custom-call | tf_op jit(solution)/shard_map/jit(cholesky)/cholesky | solution.py:48
  209.4 0.6 compare_reduce_fusion.1
  210.1 0.7 fusion.35
  210.7 4.9 custom-call.11
  215.6 1.1 fusion.59
  216.7 0.3 fusion.42
  217.0 0.2 fusion.44
  217.2 0.1 fusion.33
  217.3 0.2 convolution_bitcast_fusion.1
  217.5 67.3 %all-reduce.9.cloned.1.call-done = f32[64,2048]{1,0:T(8,128)} async-done(((f32[64,2048]{1,0:T(8,128)}), f32[64,2048]{1,0:T(8,128)}) %all-reduce.9.cloned.1.call-update) | async-done | bytes 524304 | tf_op jit(solution)/shard_map/psum | solution.py:40
  284.8 3.7 fusion.1
  288.5 3.0 fusion.2
  291.4 0.0 all-reduce.11.cloned.1.call-update
  291.4 0.0 all-reduce.13.cloned.1.call-start
  291.5 1.7 fusion.20
  293.2 0.0 all-reduce.13.cloned.1.call-update
  293.3 120.6 %all-reduce.11.cloned.1.call-done = f32[256,64]{0,1:T(8,128)} async-done(((f32[256,64]{0,1:T(8,128)}), f32[256,64]{0,1:T(8,128)}) %all-reduce.11.cloned.1.call-update) | async-done | bytes 65552 | tf_op jit(solution)/shard_map/psum | solution.py:38
  413.8 1.1 fusion.22
  414.9 57.1 %all-reduce = (f32[64,64]{1,0:T(8,128)S(1)}, f32[64]{0:T(128)S(1)}) all-reduce(f32[64,64]{1,0:T(8,128)S(1)} %fusion.22, f32[64]{0:T(128)S(1)} %convolution_bitcast_fusion.1), channel_id=1, replica_groups=mesh['line'=16,'bus'=32] {'line'}, use_global_device_ids=true, to_apply=%region_7.12 | all-reduce | flops 4160 | bytes 33280 | tf_op jit(solution)/shard_map/psum | solution.py:39
  472.0 0.2 fusion.62
  472.2 0.1 copy.12
  472.3 5.8 %cholesky.55 = f32[64,64]{1,0:T(8,128)S(1)} custom-call(f32[64,64]{1,0:T(8,128)S(1)} %fusion.41), custom_call_target="Cholesky" | custom-call | tf_op jit(solution)/shard_map/jit(cholesky)/cholesky | solution.py:48
  478.2 0.6 compare_reduce_fusion
  478.8 0.7 fusion.36
  479.5 4.9 custom-call.13
  484.4 1.1 fusion.61
  485.5 0.3 fusion.37
  485.7 0.2 fusion.39
  485.9 0.1 fusion.31
  486.1 0.6 add_multiply_fusion
  486.6 67.0 %all-reduce.13.cloned.1.call-done = f32[64,2048]{1,0:T(8,128)} async-done(((f32[64,2048]{1,0:T(8,128)}), f32[64,2048]{1,0:T(8,128)}) %all-reduce.13.cloned.1.call-update) | async-done | bytes 524304 | tf_op jit(solution)/shard_map/psum | solution.py:40
  553.6 4.3 fusion
  (11 shorter events, 0.1 us)
Async XLA Ops:
  7.2 0.9 copy-start
  7.2 7.9 %copy-start.3 = (s32[2,64]{1,0:T(2,128)S(1)}, s32[2,64]{1,0:T(2,128)}, u32[]{:S(2)}) copy-start(s32[2,64]{1,0:T(2,128)} %param.16) | copy-start | bytes 1540
  7.2 7.9 %copy-start.2 = (f32[256,2048]{1,0:T(8,128)S(1)}, f32[256,2048]{1,0:T(8,128)}, u32[]{:S(2)}) copy-start(f32[256,2048]{1,0:T(8,128)} %param.12) | copy-start | bytes 6291460
  7.2 137.9 %all-reduce.7.cloned.1.call-start = ((), (), s32[]{:S(2)}) async-start(), calls=%async_computation | async-start | bytes 131072 | tf_op jit(solution)/shard_map/psum | solution.py:38
  15.0 2.7 copy-start.1
  15.0 269.8 %all-reduce.9.cloned.1.call-start = ((), (), s32[]{:S(2)}) async-start(), calls=%async_computation.1 | async-start | bytes 1048576 | tf_op jit(solution)/shard_map/psum | solution.py:40
  15.1 3.4 copy-start.4
  16.9 397.0 %all-reduce.11.cloned.1.call-start = ((), (), s32[]{:S(2)}) async-start(), calls=%async_computation.2 | async-start | bytes 131072 | tf_op jit(solution)/shard_map/psum | solution.py:38
  291.4 262.2 %all-reduce.13.cloned.1.call-start = ((), (), s32[]{:S(2)}) async-start(), calls=%async_computation.3 | async-start | bytes 1048576 | tf_op jit(solution)/shard_map/psum | solution.py:40
Sparse Core Ops, SparseCore 0:
  15.1 129.9 all-reduce.6
  148.0 136.6 all-reduce.8
  291.6 122.2 all-reduce.10
  416.7 136.8 all-reduce.12
where the time goes:
time: 565 us; the launch traced here: 564 us
  waiting for transfers between devices  381 us (67%)
  blocking collectives  114 us (20%)
  other arithmetic  25.7 us (5%)
  matrix products  25.1 us (4%)
  between operations  14 us (2%)
    psum x2, waiting for transfers between devices, per_device(): terminal = lax.psum(terminal_part, 'bus')  247 us
    psum x2, waiting for transfers between devices, per_device(): lax.psum((jnp.dot(outage_select, factors, precision=precise), jnp.dot(out...  134 us
    psum x2, blocking collectives, per_device(): lax.psum(jnp.dot(outage_select, terminal, precision=precise), 'line')  114 us
    another operation x6, other arithmetic, per_device(): jnp.linalg.cholesky(jnp.dot(capacitance, capacitance.T, precision=precise))  13 us
  transfers between devices with their start and end apart: 4, of which 4 were waited for; matrix products, arithmetic and copies ran while one was open for 6% of the time, Pallas kernels for 0%

commit v1 on v0

v1 whole, which is shorter than its diff:
```python
import jax
import jax.numpy as jnp
from jax import lax
from jax.sharding import PartitionSpec as P

PRECISE = lax.Precision.HIGHEST


def chol_solve(factor_lower, right):
    middle = lax.linalg.triangular_solve(factor_lower, right, left_side=True, lower=True)
    return lax.linalg.triangular_solve(
        factor_lower, middle, left_side=True, lower=True, transpose_a=True
    )


def solve_weights(capacitance, terminal_rows):
    factor_lower = jnp.linalg.cholesky(jnp.dot(capacitance, capacitance.T, precision=PRECISE))
    return chol_solve(factor_lower, jnp.dot(capacitance, terminal_rows.T, precision=PRECISE))


def slot_layout(tripped, local_rows, cap):
    steps, outages = tripped.shape
    block = tripped // local_rows
    earlier = jnp.arange(outages)[None, :] < jnp.arange(outages)[:, None]
    same = (block[:, :, None] == block[:, None, :]) & earlier[None]
    rank = jnp.sum(same, axis=2).astype(jnp.int32)
    seg = jnp.arange(steps, dtype=jnp.int32)[:, None]
    slot = block * (steps * cap) + seg * cap + rank
    return block, rank, slot


def per_device(transfer_factors, line_flows, from_bus, to_bus, tripped):
    local_rows, local_cols = transfer_factors.shape
    steps, outages = tripped.shape
    cap = 8
    line_index = lax.axis_index("line")
    bus_index = lax.axis_index("bus")
    ids = tripped.reshape(-1)

    def local_column(bus):
        offset = bus - bus_index * local_cols
        inside = (offset >= 0) & (offset < local_cols)
        values = jnp.take(transfer_factors, jnp.clip(offset, 0, local_cols - 1), axis=1)
        return jnp.where(inside[None, :], values, 0.0)

    terminal_part = local_column(jnp.take(from_bus, ids)) - local_column(jnp.take(to_bus, ids))
    terminal = lax.psum(terminal_part, "bus")

    block, rank, slot = slot_layout(tripped, local_rows, cap)
    mine = (block == line_index)[:, None, :] & (
        rank[:, None, :] == jnp.arange(cap, dtype=jnp.int32)[None, :, None]
    )
    position = jnp.sum(jnp.where(mine, (tripped - line_index * local_rows)[:, None, :], 0), axis=2)
    valid = jnp.any(mine, axis=2).reshape(-1)
    position = position.reshape(-1)
    rows = jnp.where(valid[:, None], jnp.take(transfer_factors, position, axis=0), 0.0)
    small = jnp.concatenate(
        [jnp.take(terminal, position, axis=0), jnp.take(line_flows, position)[:, None]], axis=1
    )
    small = jnp.where(valid[:, None], small, 0.0)

    gathered_rows = lax.all_gather(rows, "line").reshape(-1, local_cols)
    gathered_small = lax.all_gather(small, "line").reshape(-1, small.shape[1])
    slot_flat = slot.reshape(-1)
    outage_rows = jnp.take(gathered_rows, slot_flat, axis=0)
    outage_small = jnp.take(gathered_small, slot_flat, axis=0)
    outage_terms = outage_small[:, : steps * outages]
    outage_flows = outage_small[:, steps * outages]

    identity = jnp.eye(outages, dtype=jnp.float32)
    row_global = line_index * local_rows + jnp.arange(local_rows, dtype=jnp.int32)
    hit = row_global[:, None] == tripped[0][None, :]
    keep1 = 1.0 - jnp.any(hit, axis=1).astype(jnp.float32)
    hit2 = row_global[:, None] == tripped[1][None, :]
    keep12 = keep1 * (1.0 - jnp.any(hit2, axis=1).astype(jnp.float32))

    s1 = slice(0, outages)
    s2 = slice(outages, 2 * outages)
    cap1 = identity - outage_terms[s1, s1]
    rhs1 = jnp.concatenate([terminal[:, s1], outage_terms[s2, s1]], axis=0)
    w1 = solve_weights(cap1, rhs1)
    w1t_local = w1[:, :local_rows].T
    w1t_out2 = w1[:, local_rows:].T
    terminal2 = keep1[:, None] * (
        terminal[:, s2] + jnp.dot(w1t_local, outage_terms[s1, s2], precision=PRECISE)
    )
    out2 = outage_terms[s2, s2] + jnp.dot(w1t_out2, outage_terms[s1, s2], precision=PRECISE)
    cap2 = identity - out2
    w2t = solve_weights(cap2, terminal2).T
    combined = jnp.concatenate(
        [w1t_local + jnp.dot(w2t, w1t_out2, precision=PRECISE), w2t], axis=1
    )

    factors = keep12[:, None] * (
        transfer_factors + jnp.dot(combined, outage_rows, precision=PRECISE)
    )
    flows = keep12 * (line_flows + jnp.dot(combined, outage_flows, precision=PRECISE))
    return (factors, flows)


def solution(mesh):
    placed = (P("line", "bus"), P("line"), P(), P(), P())
    return jax.shard_map(
        per_device,
        mesh=mesh,
        in_specs=placed,
        out_specs=(P("line", "bus"), P("line")),
        check_vma=False,
    )
```

time: 565 us -> 233 us (0.41)
  waiting for transfers between devices: 381 us -> 133 us
  blocking collectives: 114 us -> 31.7 us
  matrix products: 25.1 us -> 5.96 us
  local copies, waits for them, and re-layouts: 4 us -> 18.9 us
    psum x2 -> x0, waiting for transfers between devices: 134 us -> none  [per_device(): lax.psum((jnp.dot(outage_select, factors, precision=precise), jnp.dot(out...]
    psum x2 -> x0, blocking collectives: 114 us -> none  [per_device(): lax.psum(jnp.dot(outage_select, terminal, precision=precise), 'line')]
    psum x2 -> x1, waiting for transfers between devices: 247 us -> 133 us  [per_device(): terminal = lax.psum(terminal_part, 'bus')]
    all_gather x0 -> x1, blocking collectives: none -> 31.7 us  [per_device(): gathered_small = lax.all_gather(small, 'line').reshape(-1, small.shape[1])]
    dot_general x16 -> x9, matrix products: 24.2 us -> 5.01 us  [the longest x1 3.28 us: per_device(): jnp.dot(combined, outage_rows, precision=PRECISE)]
    gather x4 -> x9, local copies, waits for them, and re-layouts: 3.81 us -> 13.3 us  [the longest x2 4.83 us: local_column(): jnp.take(transfer_factors, jnp.clip(offset, 0, local_cols - 1), axis=1)]
  transfers between devices with their start and end apart: 4 -> 2, of which waited for: 4 -> 1; matrix products, arithmetic and copies ran while one was open for 6% -> 14% of each run, Pallas kernels for 0% -> 0%
where the time goes in v1:
time: 233 us
  waiting for transfers between devices  133 us (57%)
  blocking collectives  31.7 us (14%)
  other arithmetic  27.3 us (12%)
  local copies, waits for them, and re-layouts  18.9 us (8%)
  between operations  15.8 us (7%)
  matrix products  5.96 us (3%)
    psum x1, waiting for transfers between devices, per_device(): terminal = lax.psum(terminal_part, 'bus')  133 us
    all_gather x1, blocking collectives, per_device(): gathered_small = lax.all_gather(small, 'line').reshape(-1, small.shape[1])  31.7 us
    another operation x6, other arithmetic, solve_weights(): jnp.linalg.cholesky(jnp.dot(capacitance, capacitance.T, precision=PRECISE))  13 us
    another operation x4, other arithmetic, chol_solve(): lax.linalg.triangular_solve(factor_lower, middle, left_side=True, lower=T...  11.1 us
    gather x2, local copies, waits for them, and re-layouts, local_column(): jnp.take(transfer_factors, jnp.clip(offset, 0, local_cols - 1), axis=1)  4.83 us
  transfers between devices with their start and end apart: 2, of which 1 were waited for; matrix products, arithmetic and copies ran while one was open for 14% of the time, Pallas kernels for 0%

profile of v1, /device:TPU:6, one launch (start us, length us, event | category | flops | bytes accessed | tf_op | source)
XLA Modules:
  0.0 232.9 jit_solution(3203836839279586236)
XLA Ops:
  8.0 0.0 copy-start
  8.0 0.0 all-reduce.2.cloned.1.call-start
  8.1 0.8 reshape.325
  8.8 1.1 gather_fusion.5
  10.0 1.6 gather_fusion.7
  11.6 2.9 %copy.28 = f32[256,2048]{0,1:T(8,128)} copy(f32[256,2048]{1,0:T(8,128)} %param.10) | data formatting | bytes 4194304 | tf_op args[0]
  14.6 0.0 copy-start.1
  14.6 2.5 %gather_fusion.6 = f32[128,256]{1,0:T(8,128)S(1)} fusion(f32[256,2048]{0,1:T(8,128)} %copy.28, s32[1024]{0:T(1024)S(1)} %get-tuple-element.24), kind=kCustom, calls=%fused_computation.1.clone | custom fusion | bytes 262656 | tf_op jit(solution)/shard_map/jit(_take)/gather | solution.py:43
  17.1 2.3 %gather_fusion.8 = f32[128,256]{1,0:T(8,128)S(1)} fusion(f32[256,2048]{0,1:T(8,128)} %copy.28, s32[1024]{0:T(1024)S(1)} %get-tuple-element.23), kind=kCustom, calls=%fused_computation.3.clone | custom fusion | bytes 262656 | tf_op jit(solution)/shard_map/jit(_take)/gather | solution.py:43
  19.4 0.8 fusion.7
  20.2 0.0 all-reduce.2.cloned.1.call-update
  20.2 0.0 all-gather.2.cloned.1.call-start
  20.3 0.0 copy-done.4
  20.4 0.2 convert_reduce_fusion
  20.5 0.2 select_reduce_fusion.2
  20.7 0.1 reshape.326
  20.8 0.1 reshape.324
  20.9 0.2 fusion.32
  21.1 0.1 broadcast_in_dim.132
  21.1 0.6 gather_fusion.3
  21.7 0.7 fusion.6
  22.5 0.0 all-gather.2.cloned.1.call-update
  22.5 0.1 add_add_fusion
  22.6 0.1 reshape.328
  22.7 0.1 reshape.323
  22.8 0.7 gather_fusion.1
  23.4 0.1 copy.31
  23.6 0.1 compare_reduce_fusion.1
  23.7 133.1 %all-reduce.2.cloned.1.call-done = f32[256,128]{0,1:T(8,128)} async-done(((f32[256,128]{0,1:T(8,128)}), f32[256,128]{0,1:T(8,128)}) %all-reduce.2.cloned.1.call-update) | async-done | bytes 131088 | tf_op jit(solution)/shard_map/psum | solution.py:47
  156.8 1.1 copy.30
  157.9 0.6 gather_fusion
  158.5 0.1 select_bitcast_fusion
  158.6 0.1 maximum_select_fusion
  158.6 31.7 %all_gather.8 = f32[16,16,129]{2,1,0:T(8,128)S(1)} all-gather(f32[1,16,129]{2,1,0:T(8,128)S(1)} %maximum_select_fusion), channel_id=1, replica_groups=mesh['line'=16,'bus'=32] {'line'}, dimensions={0}, use_global_device_ids=true | all-gather | bytes 140352 | tf_op jit(solution)/shard_map/all_gather | solution.py:63
  190.4 0.8 gather_fusion.2
  191.1 0.1 broadcast_select_fusion
  191.2 0.2 fusion.30
  191.4 0.1 copy.32
  191.5 5.8 %cholesky.44 = f32[64,64]{1,0:T(8,128)S(1)} custom-call(f32[64,64]{1,0:T(8,128)S(1)} %fusion.25), custom_call_target="Cholesky" | custom-call | tf_op jit(solution)/shard_map/jit(cholesky)/cholesky | solution.py:17
  197.4 0.6 compare_reduce_fusion.3
  198.0 0.7 fusion.14
  198.7 4.9 %custom-call.12 = f32[1,64,64]{1,2,0:T(8,128)S(1)} custom-call(f32[1,64,64]{2,1,0:T(8,128)S(1)} %fusion.14), custom_call_target="InvertDiagBlocksLowerTriangular" | custom-call | tf_op jit(solution)/shard_map/triangular_solve | solution.py:11
  203.6 0.1 copy.33
  203.7 0.0 slice-done
  203.7 0.2 fusion.9
  203.9 0.3 fusion.23
  204.2 0.2 fusion.21
  204.4 0.3 fusion.2
  204.7 0.2 fusion.41
  204.9 0.1 copy.34
  205.0 5.8 %cholesky.55 = f32[64,64]{1,0:T(8,128)S(1)} custom-call(f32[64,64]{1,0:T(8,128)S(1)} %fusion.20), custom_call_target="Cholesky" | custom-call | tf_op jit(solution)/shard_map/jit(cholesky)/cholesky | solution.py:17
  210.9 0.6 compare_reduce_fusion.2
  211.5 0.7 fusion.15
  212.2 4.9 %custom-call.13 = f32[1,64,64]{1,2,0:T(8,128)S(1)} custom-call(f32[1,64,64]{2,1,0:T(8,128)S(1)} %fusion.15), custom_call_target="InvertDiagBlocksLowerTriangular" | custom-call | tf_op jit(solution)/shard_map/triangular_solve | solution.py:11
  217.1 0.1 slice_reduce_fusion
  217.2 0.3 fusion.1
  217.5 0.2 fusion.42
  217.7 0.3 fusion.18
  218.0 0.2 fusion.16
  218.2 0.2 convolution_add_fusion.1
  218.4 0.2 fusion.8
  218.6 0.6 add_multiply_fusion
  219.2 3.0 %gather_fusion.4 = f32[128,2048]{1,0:T(8,128)S(1)} fusion(f32[256,2048]{1,0:T(8,128)} %bitcast.68, s32[1024]{0:T(1024)S(1)} %pad_clamp_fusion), kind=kCustom, calls=%fused_computation.8 | custom fusion | bytes 2097664 | tf_op jit(solution)/shard_map/jit(_take)/gather | solution.py:65
  222.2 3.3 %fusion = f32[256,2048]{1,0:T(8,128)} fusion(f32[256,2048]{1,0:T(8,128)S(1)} %copy-done.2, f32[128,2048]{1,0:T(8,128)S(1)} %gather_fusion.4, f32[256]{0:T(256)S(1)} %get-tuple-element.16, pred[128]{0:T(512)(128)(4,1)S(1)} %compare_and_fusion.6, f32[256,64]{0,1:T(8,128)S(1)} %bitcast.71, f32[256,64]{0,1:T(8,128)S(1)} %convolution_add_fusion.1), kind=kOutput, calls=%fused_computation.10 | convolution fusion | flops 806649856 | bytes 5375104 | tf_op jit(solution)/shard_map/dot_general | solution.py:95
  (33 shorter events, 0.2 us)
Async XLA Ops:
  8.0 0.8 copy-start
  8.0 148.8 %all-reduce.2.cloned.1.call-start = ((), (), s32[]{:S(2)}) async-start(), calls=%async_computation | async-start | bytes 262144 | tf_op jit(solution)/shard_map/psum | solution.py:47
  14.5 5.8 %copy-start.4 = (s32[2,64]{1,0:T(2,128)S(1)}, s32[2,64]{1,0:T(2,128)}, u32[]{:S(2)}) copy-start(s32[2,64]{1,0:T(2,128)} %param.14) | copy-start | bytes 1540
  14.5 6.6 %copy-start.2 = (f32[256,2048]{1,0:T(8,128)S(1)}, f32[256,2048]{1,0:T(8,128)}, u32[]{:S(2)}) copy-start(f32[256,2048]{1,0:T(8,128)} %param.10) | copy-start | bytes 6291460
  14.6 8.2 %copy-start.1 = (f32[256]{0:T(256)S(1)}, f32[256]{0:T(256)}, u32[]{:S(2)}) copy-start(f32[256]{0:T(256)} %param.11) | copy-start | bytes 3076
  20.2 198.9 %all-gather.2.cloned.1.call-start = ((), (), s32[]{:S(2)}) async-start(), calls=%async_computation.1 | async-start | bytes 2228224 | tf_op jit(solution)/shard_map/all_gather | solution.py:62
  156.8 46.9 %slice-start = ((f32[256,128]{0,1:T(8,128)}), f32[256,64]{0,1:T(8,128)S(1)}, s32[]{:S(2)}) async-start(f32[256,128]{0,1:T(8,128)} %all-reduce.2.cloned.1.call-done), calls=%async_computation.2 | async-start | bytes 131072 | tf_op jit(solution)/shard_map/slice | solution.py:80
  156.8 60.4 %copy-start.3 = (f32[256,128]{0,1:T(8,128)S(1)}, f32[256,128]{0,1:T(8,128)}, u32[]{:S(2)}) copy-start(f32[256,128]{0,1:T(8,128)} %all-reduce.2.cloned.1.call-done) | copy-start | bytes 393220
Sparse Core Ops, SparseCore 0:
  20.4 136.3 all-reduce.1
Sparse Core Ops, SparseCore 1:
  23.4 77.5 all-gather.1

commit v2 on v1

--- a/solution.py
+++ b/solution.py
@@ -1,9 +1,158 @@
+import functools
+
 import jax
 import jax.numpy as jnp
 from jax import lax
+from jax.experimental import pallas as pl
+from jax.experimental.pallas import tpu as pltpu
 from jax.sharding import PartitionSpec as P
 
 PRECISE = lax.Precision.HIGHEST
+
+
+def _mesh_id(axis, peer):
+    coords = {"line": lax.axis_index("line"), "bus": lax.axis_index("bus")}
+    coords[axis] = peer
+    return (coords["line"], coords["bus"])
+
+
+def _greet(axis, n):
+    barrier = pltpu.get_barrier_semaphore()
+    me = lax.axis_index(axis)
+
+    def body(k, carry):
+        peer = lax.rem(me + k, n)
+        pl.semaphore_signal(
+            barrier, 1, device_id=_mesh_id(axis, peer), device_id_type=pl.DeviceIdType.MESH
+        )
+        return carry
+
+    lax.fori_loop(1, n, body, 0)
+    pl.semaphore_wait(barrier, n - 1)
+
+
+def _bus_reduce_kernel(n, x_ref, o_ref, recv, gathered, mine, s1, r1, s2, r2):
+    me = lax.axis_index("bus")
+    chunk = x_ref.shape[0] // n
+    _greet("bus", n)
+
+    def send1(k):
+        peer = lax.rem(me + k, n)
+        return pltpu.make_async_remote_copy(
+            src_ref=x_ref.at[pl.ds(peer * chunk, chunk)],
+            dst_ref=recv.at[k],
+            send_sem=s1.at[k],
+            recv_sem=r1.at[k],
+            device_id=_mesh_id("bus", peer),
+            device_id_type=pl.DeviceIdType.MESH,
+        )
+
+    def start1(k, carry):
+        send1(k).start()
+        return carry
+
+    lax.fori_loop(1, n, start1, 0)
+    total = x_ref[pl.ds(me * chunk, chunk), :]
+
+    def finish1(k, acc):
+        send1(k).wait()
+        return acc + recv[k]
+
+    total = lax.fori_loop(1, n, finish1, total)
+    gathered[pl.ds(me * chunk, chunk), :] = total
+    mine[...] = total
+
+    def send2(k):
+        peer = lax.rem(me + k, n)
+        return pltpu.make_async_remote_copy(
+            src_ref=mine,
+            dst_ref=gathered.at[pl.ds(me * chunk, chunk)],
+            send_sem=s2.at[k],
+            recv_sem=r2.at[k],
+            device_id=_mesh_id("bus", peer),
+            device_id_type=pl.DeviceIdType.MESH,
+        )
+
+    def start2(k, carry):
+        send2(k).start()
+        return carry
+
+    lax.fori_loop(1, n, start2, 0)
+
+    def finish2(k, carry):
+        send2(k).wait()
+        return carry
+
+    lax.fori_loop(1, n, finish2, 0)
+    o_ref[...] = gathered[...]
+
+
+def bus_reduce(x, n):
+    rows, cols = x.shape
+    chunk = rows // n
+    vmem = pl.BlockSpec(memory_space=pltpu.VMEM)
+    return pl.pallas_call(
+        functools.partial(_bus_reduce_kernel, n),
+        out_shape=jax.ShapeDtypeStruct((rows, cols), x.dtype),
+        in_specs=[vmem],
+        out_specs=vmem,
+        scratch_shapes=[
+            pltpu.VMEM((n, chunk, cols), x.dtype),
+            pltpu.VMEM((rows, cols), x.dtype),
+            pltpu.VMEM((chunk, cols), x.dtype),
+            pltpu.SemaphoreType.DMA((n,)),
+            pltpu.SemaphoreType.DMA((n,)),
+            pltpu.SemaphoreType.DMA((n,)),
+            pltpu.SemaphoreType.DMA((n,)),
+        ],
+        compiler_params=pltpu.CompilerParams(collective_id=0, has_side_effects=True),
+    )(x)
+
+
+def _line_gather_kernel(n, x_ref, o_ref, gathered, s1, r1):
+    me = lax.axis_index("line")
+    _greet("line", n)
+
+    def send(k):
+        peer = lax.rem(me + k, n)
+        return pltpu.make_async_remote_copy(
+            src_ref=x_ref,
+            dst_ref=gathered.at[me],
+            send_sem=s1.at[k],
+            recv_sem=r1.at[k],
+            device_id=_mesh_id("line", peer),
+            device_id_type=pl.DeviceIdType.MESH,
+        )
+
+    def start(k, carry):
+        send(k).start()
+        return carry
+
+    lax.fori_loop(1, n, start, 0)
+    gathered[me] = x_ref[...]
+
+    def finish(k, carry):
+        send(k).wait()
+        return carry
+
+    lax.fori_loop(1, n, finish, 0)
+    o_ref[...] = gathered[...]
+
+
+def line_gather(x, n):
+    vmem = pl.BlockSpec(memory_space=pltpu.VMEM)
+    return pl.pallas_call(
+        functools.partial(_line_gather_kernel, n),
+        out_shape=jax.ShapeDtypeStruct((n,) + x.shape, x.dtype),
+        in_specs=[vmem],
+        out_specs=vmem,
+        scratch_shapes=[
+            pltpu.VMEM((n,) + x.shape, x.dtype),
+            pltpu.SemaphoreType.DMA((n,)),
+            pltpu.SemaphoreType.DMA((n,)),
+        ],
+        compiler_params=pltpu.CompilerParams(collective_id=1, has_side_effects=True),
+    )(x)
 
 
 def chol_solve(factor_lower, right):
@@ -44,7 +193,7 @@
         return jnp.where(inside[None, :], values, 0.0)
 
     terminal_part = local_column(jnp.take(from_bus, ids)) - local_column(jnp.take(to_bus, ids))
-    terminal = lax.psum(terminal_part, "bus")
+    terminal = bus_reduce(terminal_part, lax.axis_size("bus"))
 
     block, rank, slot = slot_layout(tripped, local_rows, cap)
     mine = (block == line_index)[:, None, :] & (
@@ -55,12 +204,17 @@
     position = position.reshape(-1)
     rows = jnp.where(valid[:, None], jnp.take(transfer_factors, position, axis=0), 0.0)
     small = jnp.concatenate(
-        [jnp.take(terminal, position, axis=0), jnp.take(line_flows, position)[:, None]], axis=1
+        [
+            jnp.take(terminal, position, axis=0),
+            jnp.take(line_flows, position)[:, None],
+            jnp.zeros((position.shape[0], 127), jnp.float32),
+        ],
+        axis=1,
     )
     small = jnp.where(valid[:, None], small, 0.0)
 
     gathered_rows = lax.all_gather(rows, "line").reshape(-1, local_cols)
-    gathered_small = lax.all_gather(small, "line").reshape(-1, small.shape[1])
+    gathered_small = line_gather(small, lax.axis_size("line")).reshape(-1, small.shape[1])
     slot_flat = slot.reshape(-1)
     outage_rows = jnp.take(gathered_rows, slot_flat, axis=0)
     outage_small = jnp.take(gathered_small, slot_flat, axis=0)

time: 233 us -> 119 us (0.51)
  the two profiles are of different devices: /device:TPU:6 before, /device:TPU:1 now
where the time goes in v2:
time: 119 us
  Pallas kernels  51.7 us (43%)
  other arithmetic  29.3 us (25%)
  local copies, waits for them, and re-layouts  16.9 us (14%)
  between operations  14.4 us (12%)
  matrix products  6.22 us (5%)
    pallas_call x1, Pallas kernels, line_gather(): pl.pallas_call(functools.partial(_line_gather_kernel, n), out_shape=jax.S...  29.4 us
    pallas_call x1, Pallas kernels, bus_reduce(): pl.pallas_call(functools.partial(_bus_reduce_kernel, n), out_shape=jax.Sh...  22.3 us
    another operation x6, other arithmetic, solve_weights(): jnp.linalg.cholesky(jnp.dot(capacitance, capacitance.T, precision=PRECISE))  13 us
    another operation x4, other arithmetic, chol_solve(): lax.linalg.triangular_solve(factor_lower, middle, left_side=True, lower=T...  11.1 us
    dot_general x1, matrix products, per_device(): jnp.dot(combined, outage_rows, precision=PRECISE)  3.27 us
    gather x1, local copies, waits for them, and re-layouts, per_device(): outage_rows = jnp.take(gathered_rows, slot_flat, axis=0)  3.19 us
  transfers between devices with their start and end apart: 1, of which 0 were waited for; matrix products, arithmetic and copies ran while one was open for 34% of the time, Pallas kernels for 44%

profile of v2, /device:TPU:1, one launch (start us, length us, event | category | flops | bytes accessed | tf_op | source)
XLA Modules:
  0.0 118.6 jit_solution(476690041119886270)
XLA Ops:
  7.2 0.0 copy-start
  7.2 0.0 all-gather.2.cloned.1.call-start
  7.3 0.7 broadcast_compare_fusion
  7.9 0.7 broadcast_subtract_fusion
  8.6 0.2 convert_reduce_fusion
  8.8 0.2 select_reduce_fusion.2
  9.0 0.1 reshape.330
  9.0 0.1 reshape.237
  9.1 0.2 fusion.32
  9.3 0.1 fusion.33
  9.4 0.1 broadcast_in_dim.135
  9.5 2.2 %gather_fusion.3 = f32[16,2048]{1,0:T(8,128)S(1)} fusion(f32[256,2048]{1,0:T(8,128)} %param.10, s32[1024]{0:T(1024)S(1)} %pad_clamp_fusion.1), kind=kCustom, calls=%fused_computation.7 | custom fusion | bytes 262208 | tf_op jit(solution)/shard_map/jit(_take)/gather | solution.py:205
  11.8 0.7 fusion.10
  12.5 0.0 all-gather.2.cloned.1.call-update
  12.5 0.8 reshape.238
  13.3 1.9 %copy.38 = f32[256,2048]{0,1:T(8,128)S(1)} copy(f32[256,2048]{1,0:T(8,128)} %param.10) | data formatting | bytes 4194304 | tf_op args[0]
  15.2 0.1 add_add_fusion
  15.3 0.1 reshape.241
  15.4 0.1 reshape.236
  15.5 1.1 gather_fusion.5
  16.7 1.1 gather_fusion.7
  17.9 0.8 gather_fusion.6
  18.7 0.1 copy.39
  18.7 0.8 gather_fusion.8
  19.5 0.1 copy.41
  19.6 0.7 fusion.11.x_ref
  20.3 22.3 %shard_map.68 = f32[256,128]{1,0:T(8,128)} custom-call(f32[256,128]{1,0:T(8,128)} %fusion.11.x_ref), custom_call_target="tpu_custom_call" | custom-call | tf_op jit(solution)/shard_map/pallas_call | solution.py:94
  42.7 1.5 %gather_fusion = f32[16,128]{1,0:T(8,128)S(1)} fusion(f32[256,128]{1,0:T(8,128)} %shard_map.68, s32[1024]{0:T(1024)S(1)} %pad_clamp_fusion.1), kind=kCustom, calls=%fused_computation.4 | custom fusion | bytes 16448 | tf_op jit(solution)/shard_map/jit(_take)/gather | solution.py:208
  44.2 0.1 broadcast_select_fusion.1
  44.2 0.7 gather_fusion.1
  44.9 0.1 copy.45
  45.0 0.1 pad.6.clone
  45.1 0.7 maximum_select_fusion.x_ref
  45.8 29.4 %shard_map.69 = f32[16,16,256]{2,1,0:T(8,128)} custom-call(f32[16,256]{1,0:T(8,128)} %maximum_select_fusion.x_ref), custom_call_target="tpu_custom_call" | custom-call | tf_op jit(solution)/shard_map/pallas_call | solution.py:144
  75.2 1.7 %gather_fusion.2 = f32[128,256]{1,0:T(8,128)S(1)} fusion(f32[256,256]{1,0:T(8,128)} %bitcast.61, s32[1024]{0:T(1024)S(1)} %pad_clamp_fusion), kind=kCustom, calls=%fused_computation.6 | custom fusion | bytes 262656 | tf_op jit(solution)/shard_map/jit(_take)/gather | solution.py:220
  76.9 0.1 broadcast_select_fusion
  77.0 0.2 fusion.30
  77.2 0.1 copy.46
  77.3 5.8 %cholesky.44 = f32[64,64]{1,0:T(8,128)S(1)} custom-call(f32[64,64]{1,0:T(8,128)S(1)} %fusion.25), custom_call_target="Cholesky" | custom-call | tf_op jit(solution)/shard_map/jit(cholesky)/cholesky | solution.py:166
  83.1 0.6 compare_reduce_fusion.3
  83.8 0.7 fusion.14
  84.4 4.9 %custom-call.12 = f32[1,64,64]{1,2,0:T(8,128)S(1)} custom-call(f32[1,64,64]{2,1,0:T(8,128)S(1)} %fusion.14), custom_call_target="InvertDiagBlocksLowerTriangular" | custom-call | tf_op jit(solution)/shard_map/triangular_solve | solution.py:160
  89.3 0.0 copy-done.4
  89.4 0.3 fusion.6
  89.7 0.3 fusion.23
  90.0 0.2 fusion.21
  90.2 0.3 fusion.2
  90.5 0.2 fusion.40
  90.7 0.1 copy.47
  90.8 5.8 %cholesky.55 = f32[64,64]{1,0:T(8,128)S(1)} custom-call(f32[64,64]{1,0:T(8,128)S(1)} %fusion.20), custom_call_target="Cholesky" | custom-call | tf_op jit(solution)/shard_map/jit(cholesky)/cholesky | solution.py:166
  96.6 0.6 compare_reduce_fusion.2
  97.3 0.7 fusion.15
  97.9 4.9 %custom-call.13 = f32[1,64,64]{1,2,0:T(8,128)S(1)} custom-call(f32[1,64,64]{2,1,0:T(8,128)S(1)} %fusion.15), custom_call_target="InvertDiagBlocksLowerTriangular" | custom-call | tf_op jit(solution)/shard_map/triangular_solve | solution.py:160
  102.9 0.1 slice_reduce_fusion
  103.0 0.1 compare_reduce_fusion.1
  103.1 0.4 fusion.1
  103.5 0.3 fusion.41
  103.8 0.3 fusion.18
  104.1 0.2 fusion.16
  104.3 0.2 convolution_add_fusion.2
  104.5 0.2 fusion.12
  104.6 0.6 add_multiply_fusion
  105.2 3.2 %gather_fusion.4 = f32[128,2048]{1,0:T(8,128)S(1)} fusion(f32[256,2048]{1,0:T(8,128)} %bitcast.60, s32[1024]{0:T(1024)S(1)} %pad_clamp_fusion), kind=kCustom, calls=%fused_computation.8 | custom fusion | bytes 2097664 | tf_op jit(solution)/shard_map/jit(_take)/gather | solution.py:219
  108.4 3.3 %fusion = f32[256,2048]{1,0:T(8,128)} fusion(f32[256,2048]{1,0:T(8,128)S(1)} %copy-done.3, f32[128,2048]{1,0:T(8,128)S(1)} %gather_fusion.4, f32[256]{0:T(256)S(1)} %get-tuple-element.16, pred[128]{0:T(512)(128)(4,1)S(1)} %compare_and_fusion.6, f32[256,64]{0,1:T(8,128)S(1)} %bitcast.64, f32[256,64]{0,1:T(8,128)S(1)} %convolution_add_fusion.2), kind=kOutput, calls=%fused_computation.10 | convolution fusion | flops 806649856 | bytes 5375104 | tf_op jit(solution)/shard_map/dot_general | solution.py:249
  (33 shorter events, 0.2 us)
Async XLA Ops:
  7.2 8.3 %copy-start = (s32[4096]{0:T(1024)S(1)}, s32[4096]{0:T(1024)}, u32[]{:S(2)}) copy-start(s32[4096]{0:T(1024)} %param.12) | copy-start | bytes 49156
  7.2 98.1 %all-gather.2.cloned.1.call-start = ((), (), s32[]{:S(2)}) async-start(), calls=%async_computation | async-start | bytes 2228224 | tf_op jit(solution)/shard_map/all_gather | solution.py:216
  13.3 3.4 %copy-start.2 = (s32[4096]{0:T(1024)S(1)}, s32[4096]{0:T(1024)}, u32[]{:S(2)}) copy-start(s32[4096]{0:T(1024)} %param.13) | copy-start | bytes 49156
  16.7 27.6 %copy-start.1 = (f32[256]{0:T(256)S(1)}, f32[256]{0:T(256)}, u32[]{:S(2)}) copy-start(f32[256]{0:T(256)} %param.11) | copy-start | bytes 3076
  42.6 46.7 %copy-start.4 = (f32[256,128]{1,0:T(8,128)S(1)}, f32[256,128]{1,0:T(8,128)}, u32[]{:S(2)}) copy-start(f32[256,128]{1,0:T(8,128)} %shard_map.68) | copy-start | bytes 393220
  42.6 60.3 %copy-start.5 = (s32[2,64]{1,0:T(2,128)S(1)}, s32[2,64]{1,0:T(2,128)}, u32[]{:S(2)}) copy-start(s32[2,64]{1,0:T(2,128)} %param.14) | copy-start | bytes 1540
  105.2 3.2 %copy-start.3 = (f32[256,2048]{1,0:T(8,128)S(1)}, f32[256,2048]{1,0:T(8,128)}, u32[]{:S(2)}) copy-start(f32[256,2048]{1,0:T(8,128)} %param.10) | copy-start | bytes 6291460
Sparse Core Ops, SparseCore 0:
  12.6 78.3 all-gather.1

commit v3 on v2

--- a/solution.py
+++ b/solution.py
@@ -31,82 +31,134 @@
     pl.semaphore_wait(barrier, n - 1)
 
 
-def _bus_reduce_kernel(n, x_ref, o_ref, recv, gathered, mine, s1, r1, s2, r2):
+def _remote(src, dst, send_sem, recv_sem, axis, peer):
+    return pltpu.make_async_remote_copy(
+        src_ref=src,
+        dst_ref=dst,
+        send_sem=send_sem,
+        recv_sem=recv_sem,
+        device_id=_mesh_id(axis, peer),
+        device_id_type=pl.DeviceIdType.MESH,
+    )
+
+
+def _exchange_kernel(
+    n_bus, n_line, x_ref, rows_ref, o_ref, o_rows, recv, gathered, mine, held,
+    s1, r1, s2, r2, sr, rr, sl, rl,
+):
     me = lax.axis_index("bus")
-    chunk = x_ref.shape[0] // n
-    _greet("bus", n)
-
-    def send1(k):
-        peer = lax.rem(me + k, n)
-        return pltpu.make_async_remote_copy(
-            src_ref=x_ref.at[pl.ds(peer * chunk, chunk)],
-            dst_ref=recv.at[k],
-            send_sem=s1.at[k],
-            recv_sem=r1.at[k],
-            device_id=_mesh_id("bus", peer),
+    here = lax.axis_index("line")
+    right = lax.rem(here + 1, n_line)
+    left = lax.rem(here + n_line - 1, n_line)
+    chunk = x_ref.shape[0] // n_bus
+    to_right = n_line // 2
+    to_left = n_line - 1 - to_right
+
+    barrier = pltpu.get_barrier_semaphore()
+
+    def greet(k, carry):
+        pl.semaphore_signal(
+            barrier, 1, device_id=_mesh_id("bus", lax.rem(me + k, n_bus)),
             device_id_type=pl.DeviceIdType.MESH,
         )
+        return carry
+
+    lax.fori_loop(1, n_bus, greet, 0)
+    for neighbour in (left, right):
+        pl.semaphore_signal(
+            barrier, 1, device_id=_mesh_id("line", neighbour), device_id_type=pl.DeviceIdType.MESH
+        )
+    pl.semaphore_wait(barrier, n_bus - 1 + 2)
+
+    def ring(step):
+        copies = []
+        if step <= to_right:
+            origin = lax.rem(here - (step - 1) + n_line, n_line)
+            src = rows_ref if step == 1 else held.at[origin]
+            copies.append(_remote(src, held.at[origin], sr.at[step - 1], rr.at[step - 1], "line", right))
+        if step <= to_left:
+            origin = lax.rem(here + (step - 1), n_line)
+            src = rows_ref if step == 1 else held.at[origin]
+            copies.append(_remote(src, held.at[origin], sl.at[step - 1], rl.at[step - 1], "line", left))
+        return copies
+
+    first = ring(1)
+    for copy in first:
+        copy.start()
+
+    def send1(k):
+        peer = lax.rem(me + k, n_bus)
+        return _remote(x_ref.at[pl.ds(peer * chunk, chunk)], recv.at[k], s1.at[k], r1.at[k], "bus", peer)
 
     def start1(k, carry):
         send1(k).start()
         return carry
 
-    lax.fori_loop(1, n, start1, 0)
+    lax.fori_loop(1, n_bus, start1, 0)
+    held[here] = rows_ref[...]
     total = x_ref[pl.ds(me * chunk, chunk), :]
 
     def finish1(k, acc):
         send1(k).wait()
         return acc + recv[k]
 
-    total = lax.fori_loop(1, n, finish1, total)
+    total = lax.fori_loop(1, n_bus, finish1, total)
     gathered[pl.ds(me * chunk, chunk), :] = total
     mine[...] = total
 
     def send2(k):
-        peer = lax.rem(me + k, n)
-        return pltpu.make_async_remote_copy(
-            src_ref=mine,
-            dst_ref=gathered.at[pl.ds(me * chunk, chunk)],
-            send_sem=s2.at[k],
-            recv_sem=r2.at[k],
-            device_id=_mesh_id("bus", peer),
-            device_id_type=pl.DeviceIdType.MESH,
-        )
+        peer = lax.rem(me + k, n_bus)
+        return _remote(mine, gathered.at[pl.ds(me * chunk, chunk)], s2.at[k], r2.at[k], "bus", peer)
 
     def start2(k, carry):
         send2(k).start()
         return carry
 
-    lax.fori_loop(1, n, start2, 0)
+    lax.fori_loop(1, n_bus, start2, 0)
+
+    for copy in first:
+        copy.wait()
+    for step in range(2, to_right + 1):
+        copies = ring(step)
+        for copy in copies:
+            copy.start()
+        for copy in copies:
+            copy.wait()
 
     def finish2(k, carry):
         send2(k).wait()
         return carry
 
-    lax.fori_loop(1, n, finish2, 0)
+    lax.fori_loop(1, n_bus, finish2, 0)
     o_ref[...] = gathered[...]
-
-
-def bus_reduce(x, n):
-    rows, cols = x.shape
-    chunk = rows // n
+    o_rows[...] = held[...]
+
+
+def exchange(x, rows, n_bus, n_line):
+    x_rows, x_cols = x.shape
+    chunk = x_rows // n_bus
     vmem = pl.BlockSpec(memory_space=pltpu.VMEM)
+    held_shape = (n_line,) + rows.shape
     return pl.pallas_call(
-        functools.partial(_bus_reduce_kernel, n),
-        out_shape=jax.ShapeDtypeStruct((rows, cols), x.dtype),
-        in_specs=[vmem],
-        out_specs=vmem,
+        functools.partial(_exchange_kernel, n_bus, n_line),
+        out_shape=(
+            jax.ShapeDtypeStruct(x.shape, x.dtype),
+            jax.ShapeDtypeStruct(held_shape, rows.dtype),
+        ),
+        in_specs=[vmem, vmem],
+        out_specs=(vmem, vmem),
         scratch_shapes=[
-            pltpu.VMEM((n, chunk, cols), x.dtype),
-            pltpu.VMEM((rows, cols), x.dtype),
-            pltpu.VMEM((chunk, cols), x.dtype),
-            pltpu.SemaphoreType.DMA((n,)),
-            pltpu.SemaphoreType.DMA((n,)),
-            pltpu.SemaphoreType.DMA((n,)),
-            pltpu.SemaphoreType.DMA((n,)),
-        ],
-        compiler_params=pltpu.CompilerParams(collective_id=0, has_side_effects=True),
-    )(x)
+            pltpu.VMEM((n_bus, chunk, x_cols), x.dtype),
+            pltpu.VMEM(x.shape, x.dtype),
+            pltpu.VMEM((chunk, x_cols), x.dtype),
+            pltpu.VMEM(held_shape, rows.dtype),
+        ]
+        + [pltpu.SemaphoreType.DMA((n_bus,))] * 4
+        + [pltpu.SemaphoreType.DMA((n_line,))] * 4,
+        compiler_params=pltpu.CompilerParams(
+            collective_id=0, has_side_effects=True, vmem_limit_bytes=48 * 1024 * 1024
+        ),
+    )(x, rows)
 
 
 def _line_gather_kernel(n, x_ref, o_ref, gathered, s1, r1):
@@ -193,7 +245,6 @@
         return jnp.where(inside[None, :], values, 0.0)
 
     terminal_part = local_column(jnp.take(from_bus, ids)) - local_column(jnp.take(to_bus, ids))
-    terminal = bus_reduce(terminal_part, lax.axis_size("bus"))
 
     block, rank, slot = slot_layout(tripped, local_rows, cap)
     mine = (block == line_index)[:, None, :] & (
@@ -203,6 +254,10 @@
     valid = jnp.any(mine, axis=2).reshape(-1)
     position = position.reshape(-1)
     rows = jnp.where(valid[:, None], jnp.take(transfer_factors, position, axis=0), 0.0)
+    terminal, gathered_rows = exchange(
+        terminal_part, rows, lax.axis_size("bus"), lax.axis_size("line")
+    )
+    gathered_rows = gathered_rows.reshape(-1, local_cols)
     small = jnp.concatenate(
         [
             jnp.take(terminal, position, axis=0),
@@ -213,7 +268,6 @@
     )
     small = jnp.where(valid[:, None], small, 0.0)
 
-    gathered_rows = lax.all_gather(rows, "line").reshape(-1, local_cols)
     gathered_small = line_gather(small, lax.axis_size("line")).reshape(-1, small.shape[1])
     slot_flat = slot.reshape(-1)
     outage_rows = jnp.take(gathered_rows, slot_flat, axis=0)

time: 119 us -> 128 us (1.076)
  the two profiles are of different devices: /device:TPU:1 before, /device:TPU:6 now
where the time goes in v3:
time: 128 us; the launch traced here: 127 us
  Pallas kernels  75.1 us (59%)
  other arithmetic  26.6 us (21%)
  local copies, waits for them, and re-layouts  16.8 us (13%)
  matrix products  7.83 us (6%)
    pallas_call x1, Pallas kernels, exchange(): pl.pallas_call(functools.partial(_exchange_kernel, n_bus, n_line), out_sh...  55.8 us
    pallas_call x1, Pallas kernels, line_gather(): pl.pallas_call(functools.partial(_line_gather_kernel, n), out_shape=jax.S...  19.4 us
    another operation x6, other arithmetic, solve_weights(): jnp.linalg.cholesky(jnp.dot(capacitance, capacitance.T, precision=PRECISE))  13 us
    another operation x4, other arithmetic, chol_solve(): lax.linalg.triangular_solve(factor_lower, middle, left_side=True, lower=T...  11.1 us
    gather x4, local copies, waits for them, and re-layouts, local_column(): jnp.take(transfer_factors, jnp.clip(offset, 0, local_cols - 1), axis=1)  5.02 us
    dot_general x1, matrix products, per_device(): jnp.dot(combined, outage_rows, precision=PRECISE)  4.87 us
    unnamed x9, local copies, waits for them, and re-layouts  2.91 us

profile of v3, /device:TPU:6, one launch (start us, length us, event | category | flops | bytes accessed | tf_op | source)
XLA Modules:
  0.0 127.4 jit_solution(889365673323889140)
XLA Ops:
  0.6 0.0 copy-start
  0.6 0.8 reshape.184
  1.4 0.0 copy-done
  1.4 1.1 gather_fusion.5
  2.6 1.6 %gather_fusion.7 = s32[128]{0:T(128)S(1)} fusion(s32[4096]{0:T(1024)} %param.13, s32[1024]{0:T(1024)S(1)} %pad_clamp_fusion.4), kind=kCustom, calls=%fused_computation.2.clone | custom fusion | bytes 1536 | tf_op jit(solution)/shard_map/jit(_take)/gather | solution.py:247
  4.3 2.9 %copy.27 = f32[256,2048]{0,1:T(8,128)} copy(f32[256,2048]{1,0:T(8,128)} %param.10) | data formatting | bytes 4194304 | tf_op args[0]
  7.2 0.0 copy-start.3
  7.2 2.5 %gather_fusion.6 = f32[128,256]{1,0:T(8,128)S(1)} fusion(f32[256,2048]{0,1:T(8,128)} %copy.27, s32[1024]{0:T(1024)S(1)} %get-tuple-element.28), kind=kCustom, calls=%fused_computation.1.clone | custom fusion | bytes 262656 | tf_op jit(solution)/shard_map/jit(_take)/gather | solution.py:244
  9.7 0.0 copy-start.1
  9.7 0.1 copy.28
  9.8 2.3 %gather_fusion.8 = f32[128,256]{1,0:T(8,128)S(1)} fusion(f32[256,2048]{0,1:T(8,128)} %copy.27, s32[1024]{0:T(1024)S(1)} %get-tuple-element.27), kind=kCustom, calls=%fused_computation.3.clone | custom fusion | bytes 262656 | tf_op jit(solution)/shard_map/jit(_take)/gather | solution.py:244
  12.1 0.1 copy.30
  12.3 0.0 copy-done.3
  12.3 0.2 convert_reduce_fusion
  12.5 0.1 select_reduce_fusion.2
  12.7 0.1 reshape.276
  12.7 0.1 fusion.32
  12.9 0.0 copy-done.2
  12.9 0.6 gather_fusion
  13.5 0.1 reshape.183
  13.6 0.1 fusion.31
  13.7 0.1 broadcast_in_dim.135
  13.8 0.1 select_select_fusion.rows_ref
  13.9 55.8 %shard_map.68 = (f32[256,128]{1,0:T(8,128)S(1)}, f32[16,16,2048]{2,1,0:T(8,128)S(1)}) custom-call(f32[256,128]{1,0:T(8,128)S(1)} %fusion.10.x_ref, f32[16,2048]{1,0:T(8,128)S(1)} %select_select_fusion.rows_ref), custom_call_target="tpu_custom_call" | custom-call | tf_op jit(solution)/shard_map/pallas_call | solution.py:142
  69.7 0.6 gather_fusion.1
  70.3 0.1 broadcast_select_fusion.1
  70.3 0.0 copy-done.1
  70.3 0.7 gather_fusion.2
  71.0 0.1 copy.34
  71.1 0.1 pad.6.clone
  71.2 0.7 maximum_select_fusion.x_ref
  71.9 19.4 %shard_map.69 = f32[16,16,256]{2,1,0:T(8,128)} custom-call(f32[16,256]{1,0:T(8,128)} %maximum_select_fusion.x_ref), custom_call_target="tpu_custom_call" | custom-call | tf_op jit(solution)/shard_map/pallas_call | solution.py:196
  91.2 0.1 add_add_fusion
  91.3 0.1 reshape.187
  91.4 1.7 %gather_fusion.3 = f32[128,256]{1,0:T(8,128)S(1)} fusion(f32[256,256]{1,0:T(8,128)} %bitcast.58, s32[1024]{0:T(1024)S(1)} %pad_clamp_fusion), kind=kCustom, calls=%fused_computation.7 | custom fusion | bytes 262656 | tf_op jit(solution)/shard_map/jit(_take)/gather | solution.py:274
  93.1 0.1 reshape.182
  93.2 0.1 broadcast_select_fusion
  93.3 0.2 fusion.29
  93.5 0.1 copy.35
  93.6 5.8 %cholesky.44 = f32[64,64]{1,0:T(8,128)S(1)} custom-call(f32[64,64]{1,0:T(8,128)S(1)} %fusion.24), custom_call_target="Cholesky" | custom-call | tf_op jit(solution)/shard_map/jit(cholesky)/cholesky | solution.py:218
  99.5 0.6 compare_reduce_fusion.3
  100.1 0.7 fusion.13
  100.8 4.9 %custom-call.12 = f32[1,64,64]{1,2,0:T(8,128)S(1)} custom-call(f32[1,64,64]{2,1,0:T(8,128)S(1)} %fusion.13), custom_call_target="InvertDiagBlocksLowerTriangular" | custom-call | tf_op jit(solution)/shard_map/triangular_solve | solution.py:212
  105.7 0.3 fusion.6
  106.0 0.3 fusion.22
  106.3 0.2 fusion.20
  106.5 0.3 fusion.2
  106.8 0.2 fusion.39
  107.0 0.1 copy.36
  107.1 5.8 %cholesky.55 = f32[64,64]{1,0:T(8,128)S(1)} custom-call(f32[64,64]{1,0:T(8,128)S(1)} %fusion.19), custom_call_target="Cholesky" | custom-call | tf_op jit(solution)/shard_map/jit(cholesky)/cholesky | solution.py:218
  113.0 0.6 compare_reduce_fusion.2
  113.6 0.7 fusion.14
  114.3 4.9 %custom-call.13 = f32[1,64,64]{1,2,0:T(8,128)S(1)} custom-call(f32[1,64,64]{2,1,0:T(8,128)S(1)} %fusion.14), custom_call_target="InvertDiagBlocksLowerTriangular" | custom-call | tf_op jit(solution)/shard_map/triangular_solve | solution.py:212
  119.2 0.1 compare_reduce_fusion.1
  119.3 0.4 fusion.1
  119.8 0.3 fusion.40
  120.0 0.3 fusion.17
  120.3 0.2 fusion.15
  120.5 0.2 convolution_add_fusion.2
  120.7 0.1 slice_reduce_fusion
  120.8 0.2 fusion.11
  121.0 0.6 add_multiply_fusion
  121.6 1.0 gather_fusion.4
  122.5 4.9 %fusion = f32[256,2048]{1,0:T(8,128)} fusion(f32[256,2048]{1,0:T(8,128)} %param.10, f32[128,2048]{1,0:T(8,128)S(1)} %gather_fusion.4, f32[256]{0:T(256)S(1)} %get-tuple-element.20, pred[128]{0:T(512)(128)(4,1)S(1)} %compare_and_fusion.6, f32[256,64]{0,1:T(8,128)S(1)} %bitcast.60, f32[256,64]{0,1:T(8,128)S(1)} %convolution_add_fusion.2), kind=kOutput, calls=%fused_computation.10 | convolution fusion | flops 806649856 | bytes 5375104 | tf_op jit(solution)/shard_map/dot_general | solution.py:303
  (26 shorter events, 0.3 us)
Async XLA Ops:
  0.6 0.8 copy-start
  7.2 5.1 %copy-start.3 = (s32[2,64]{1,0:T(2,128)S(1)}, s32[2,64]{1,0:T(2,128)}, u32[]{:S(2)}) copy-start(s32[2,64]{1,0:T(2,128)} %param.14) | copy-start | bytes 1540
  7.2 5.7 %copy-start.2 = (f32[256,2048]{1,0:T(8,128)S(1)}, f32[256,2048]{1,0:T(8,128)}, u32[]{:S(2)}) copy-start(f32[256,2048]{1,0:T(8,128)} %param.10) | copy-start | bytes 6291460
  9.7 60.7 %copy-start.1 = (f32[256]{0:T(256)S(1)}, f32[256]{0:T(256)}, u32[]{:S(2)}) copy-start(f32[256]{0:T(256)} %param.11) | copy-start | bytes 3076

commit v4 on v3

--- a/solution.py
+++ b/solution.py
@@ -43,48 +43,57 @@
 
 
 def _exchange_kernel(
-    n_bus, n_line, x_ref, rows_ref, o_ref, o_rows, recv, gathered, mine, held,
-    s1, r1, s2, r2, sr, rr, sl, rl,
+    n_bus, n_line, pieces, pick_ref, x_ref, rows_ref, o_ref, o_rows, o_small,
+    recv, gathered, mine, held, picked, got, s1, r1, s2, r2, sr, rr, sl, rl, s3, r3,
 ):
     me = lax.axis_index("bus")
     here = lax.axis_index("line")
     right = lax.rem(here + 1, n_line)
     left = lax.rem(here + n_line - 1, n_line)
     chunk = x_ref.shape[0] // n_bus
+    piece = rows_ref.shape[0] // pieces
     to_right = n_line // 2
     to_left = n_line - 1 - to_right
+    mesh_type = pl.DeviceIdType.MESH
 
     barrier = pltpu.get_barrier_semaphore()
 
-    def greet(k, carry):
+    def greet_bus(k, carry):
         pl.semaphore_signal(
-            barrier, 1, device_id=_mesh_id("bus", lax.rem(me + k, n_bus)),
-            device_id_type=pl.DeviceIdType.MESH,
+            barrier, 1, device_id=_mesh_id("bus", lax.rem(me + k, n_bus)), device_id_type=mesh_type
         )
         return carry
 
-    lax.fori_loop(1, n_bus, greet, 0)
-    for neighbour in (left, right):
+    def greet_line(k, carry):
         pl.semaphore_signal(
-            barrier, 1, device_id=_mesh_id("line", neighbour), device_id_type=pl.DeviceIdType.MESH
+            barrier, 1, device_id=_mesh_id("line", lax.rem(here + k, n_line)),
+            device_id_type=mesh_type,
         )
-    pl.semaphore_wait(barrier, n_bus - 1 + 2)
-
-    def ring(step):
-        copies = []
-        if step <= to_right:
+        return carry
+
+    lax.fori_loop(1, n_bus, greet_bus, 0)
+    lax.fori_loop(1, n_line, greet_line, 0)
+    pl.semaphore_wait(barrier, n_bus - 1 + n_line - 1)
+
+    def ring(step, part, toward):
+        if toward == "right":
             origin = lax.rem(here - (step - 1) + n_line, n_line)
-            src = rows_ref if step == 1 else held.at[origin]
-            copies.append(_remote(src, held.at[origin], sr.at[step - 1], rr.at[step - 1], "line", right))
-        if step <= to_left:
+            peer, send_sem, recv_sem = right, sr, rr
+        else:
             origin = lax.rem(here + (step - 1), n_line)
-            src = rows_ref if step == 1 else held.at[origin]
-            copies.append(_remote(src, held.at[origin], sl.at[step - 1], rl.at[step - 1], "line", left))
-        return copies
-
-    first = ring(1)
-    for copy in first:
-        copy.start()
+            peer, send_sem, recv_sem = left, sl, rl
+        rows = pl.ds(part * piece, piece)
+        src = rows_ref.at[rows] if step == 1 else held.at[origin, rows]
+        slot = (step - 1) * pieces + part
+        return _remote(src, held.at[origin, rows], send_sem.at[slot], recv_sem.at[slot], "line", peer)
+
+    def ring_steps(toward):
+        return to_right if toward == "right" else to_left
+
+    for part in range(pieces):
+        for toward in ("right", "left"):
+            if ring_steps(toward) >= 1:
+                ring(1, part, toward).start()
 
     def send1(k):
         peer = lax.rem(me + k, n_bus)
@@ -116,95 +125,83 @@
 
     lax.fori_loop(1, n_bus, start2, 0)
 
-    for copy in first:
-        copy.wait()
     for step in range(2, to_right + 1):
-        copies = ring(step)
-        for copy in copies:
-            copy.start()
-        for copy in copies:
-            copy.wait()
+        for part in range(pieces):
+            for toward in ("right", "left"):
+                if step <= ring_steps(toward):
+                    ring(step - 1, part, toward).wait_recv()
+                    ring(step, part, toward).start()
 
     def finish2(k, carry):
         send2(k).wait()
         return carry
 
     lax.fori_loop(1, n_bus, finish2, 0)
+
+    for i in range(picked.shape[0]):
+        picked[pl.ds(i, 1), :] = gathered[pl.ds(pick_ref[i], 1), :]
+    got[here] = picked[...]
+
+    def send3(k):
+        peer = lax.rem(here + k, n_line)
+        return _remote(picked, got.at[here], s3.at[k], r3.at[k], "line", peer)
+
+    def start3(k, carry):
+        send3(k).start()
+        return carry
+
+    lax.fori_loop(1, n_line, start3, 0)
+
+    for toward in ("right", "left"):
+        last = ring_steps(toward)
+        for part in range(pieces):
+            if last >= 1:
+                ring(last, part, toward).wait_recv()
+        for step in range(1, last + 1):
+            for part in range(pieces):
+                ring(step, part, toward).wait_send()
+
+    def finish3(k, carry):
+        send3(k).wait()
+        return carry
+
+    lax.fori_loop(1, n_line, finish3, 0)
     o_ref[...] = gathered[...]
     o_rows[...] = held[...]
-
-
-def exchange(x, rows, n_bus, n_line):
+    o_small[...] = got[...]
+
+
+def exchange(pick, x, rows, n_bus, n_line, pieces=2):
     x_rows, x_cols = x.shape
     chunk = x_rows // n_bus
     vmem = pl.BlockSpec(memory_space=pltpu.VMEM)
+    smem = pl.BlockSpec(memory_space=pltpu.SMEM)
     held_shape = (n_line,) + rows.shape
+    got_shape = (n_line, pick.shape[0], x_cols)
     return pl.pallas_call(
-        functools.partial(_exchange_kernel, n_bus, n_line),
+        functools.partial(_exchange_kernel, n_bus, n_line, pieces),
         out_shape=(
             jax.ShapeDtypeStruct(x.shape, x.dtype),
             jax.ShapeDtypeStruct(held_shape, rows.dtype),
+            jax.ShapeDtypeStruct(got_shape, x.dtype),
         ),
-        in_specs=[vmem, vmem],
-        out_specs=(vmem, vmem),
+        in_specs=[smem, vmem, vmem],
+        out_specs=(vmem, vmem, vmem),
         scratch_shapes=[
             pltpu.VMEM((n_bus, chunk, x_cols), x.dtype),
             pltpu.VMEM(x.shape, x.dtype),
             pltpu.VMEM((chunk, x_cols), x.dtype),
             pltpu.VMEM(held_shape, rows.dtype),
+            pltpu.VMEM((pick.shape[0], x_cols), x.dtype),
+            pltpu.VMEM(got_shape, x.dtype),
         ]
         + [pltpu.SemaphoreType.DMA((n_bus,))] * 4
-        + [pltpu.SemaphoreType.DMA((n_line,))] * 4,
+        + [pltpu.SemaphoreType.DMA((n_line * pieces,))] * 4
+        + [pltpu.SemaphoreType.DMA((n_line,))] * 2,
         compiler_params=pltpu.CompilerParams(
             collective_id=0, has_side_effects=True, vmem_limit_bytes=48 * 1024 * 1024
         ),
-    )(x, rows)
-
-
-def _line_gather_kernel(n, x_ref, o_ref, gathered, s1, r1):
-    me = lax.axis_index("line")
-    _greet("line", n)
-
-    def send(k):
-        peer = lax.rem(me + k, n)
-        return pltpu.make_async_remote_copy(
-            src_ref=x_ref,
-            dst_ref=gathered.at[me],
-            send_sem=s1.at[k],
-            recv_sem=r1.at[k],
-            device_id=_mesh_id("line", peer),
-            device_id_type=pl.DeviceIdType.MESH,
-        )
-
-    def start(k, carry):
-        send(k).start()
-        return carry
-
-    lax.fori_loop(1, n, start, 0)
-    gathered[me] = x_ref[...]
-
-    def finish(k, carry):
-        send(k).wait()
-        return carry
-
-    lax.fori_loop(1, n, finish, 0)
-    o_ref[...] = gathered[...]
-
-
-def line_gather(x, n):
-    vmem = pl.BlockSpec(memory_space=pltpu.VMEM)
-    return pl.pallas_call(
-        functools.partial(_line_gather_kernel, n),
-        out_shape=jax.ShapeDtypeStruct((n,) + x.shape, x.dtype),
-        in_specs=[vmem],
-        out_specs=vmem,
-        scratch_shapes=[
-            pltpu.VMEM((n,) + x.shape, x.dtype),
-            pltpu.SemaphoreType.DMA((n,)),
-            pltpu.SemaphoreType.DMA((n,)),
-        ],
-        compiler_params=pltpu.CompilerParams(collective_id=1, has_side_effects=True),
-    )(x)
+    )(pick, x, rows)
 
 
 def chol_solve(factor_lower, right):
@@ -253,27 +250,21 @@
     position = jnp.sum(jnp.where(mine, (tripped - line_index * local_rows)[:, None, :], 0), axis=2)
     valid = jnp.any(mine, axis=2).reshape(-1)
     position = position.reshape(-1)
-    rows = jnp.where(valid[:, None], jnp.take(transfer_factors, position, axis=0), 0.0)
-    terminal, gathered_rows = exchange(
-        terminal_part, rows, lax.axis_size("bus"), lax.axis_size("line")
-    )
-    gathered_rows = gathered_rows.reshape(-1, local_cols)
-    small = jnp.concatenate(
-        [
-            jnp.take(terminal, position, axis=0),
-            jnp.take(line_flows, position)[:, None],
-            jnp.zeros((position.shape[0], 127), jnp.float32),
-        ],
-        axis=1,
-    )
-    small = jnp.where(valid[:, None], small, 0.0)
-
-    gathered_small = line_gather(small, lax.axis_size("line")).reshape(-1, small.shape[1])
+    rows = jnp.take(transfer_factors, position, axis=0)
+    flows = jnp.take(line_flows, position)
+    extra = jnp.zeros((position.shape[0], 128), jnp.float32).at[:, 0].set(flows)
+    rows = jnp.where(valid[:, None], jnp.concatenate([rows, extra], axis=1), 0.0)
+    pick = jnp.where(valid, position, 0).astype(jnp.int32)
+    terminal, gathered_rows, gathered_small = exchange(
+        pick, terminal_part, rows, lax.axis_size("bus"), lax.axis_size("line")
+    )
+    gathered_rows = gathered_rows.reshape(-1, rows.shape[1])
+    gathered_small = gathered_small.reshape(-1, terminal.shape[1])
     slot_flat = slot.reshape(-1)
-    outage_rows = jnp.take(gathered_rows, slot_flat, axis=0)
-    outage_small = jnp.take(gathered_small, slot_flat, axis=0)
-    outage_terms = outage_small[:, : steps * outages]
-    outage_flows = outage_small[:, steps * outages]
+    outage_all = jnp.take(gathered_rows, slot_flat, axis=0)
+    outage_rows = outage_all[:, :local_cols]
+    outage_flows = outage_all[:, local_cols]
+    outage_terms = jnp.take(gathered_small, slot_flat, axis=0)
 
     identity = jnp.eye(outages, dtype=jnp.float32)
     row_global = line_index * local_rows + jnp.arange(local_rows, dtype=jnp.int32)

time: 128 us -> 112 us (0.88)
  Pallas kernels: 75.1 us -> 60.2 us
  matrix products: 7.83 us -> 6.21 us
    pallas_call x2 -> x1, Pallas kernels: 75.1 us -> 60.2 us  [exchange(): pl.pallas_call(functools.partial(_exchange_kernel, n_bus, n_line, pieces)...]
    dot_general x1, matrix products: 4.87 us -> 3.24 us  [per_device(): jnp.dot(combined, outage_rows, precision=PRECISE)]
    gather x6 -> x5, local copies, waits for them, and re-layouts: 4.59 us -> 3.07 us  [the longest x1 1.07 us: per_device(): outage_all = jnp.take(gathered_rows, slot_flat, axis=0)]
    another operation x0 -> x2, other arithmetic: none -> 1.29 us
    unnamed x9 -> x11, local copies, waits for them, and re-layouts: 2.91 us -> 3.48 us
where the time goes in v4:
time: 112 us; the launch traced here: 111 us
  Pallas kernels  60.2 us (54%)
  other arithmetic  27.4 us (24%)
  local copies, waits for them, and re-layouts  15.8 us (14%)
  matrix products  6.21 us (6%)
    pallas_call x1, Pallas kernels, exchange(): pl.pallas_call(functools.partial(_exchange_kernel, n_bus, n_line, pieces)...  60.2 us
    another operation x6, other arithmetic, solve_weights(): jnp.linalg.cholesky(jnp.dot(capacitance, capacitance.T, precision=PRECISE))  13 us
    another operation x4, other arithmetic, chol_solve(): lax.linalg.triangular_solve(factor_lower, middle, left_side=True, lower=T...  11.1 us
    gather x4, local copies, waits for them, and re-layouts, local_column(): jnp.take(transfer_factors, jnp.clip(offset, 0, local_cols - 1), axis=1)  5.02 us
    unnamed x11, local copies, waits for them, and re-layouts  3.48 us
    dot_general x1, matrix products, per_device(): jnp.dot(combined, outage_rows, precision=PRECISE)  3.24 us

profile of v4, /device:TPU:6, one launch (start us, length us, event | category | flops | bytes accessed | tf_op | source)
XLA Modules:
  0.0 110.6 jit_solution(1046448460826328896)
XLA Ops:
  0.6 0.0 copy-start
  0.6 0.8 reshape.208
  1.4 0.0 copy-done
  1.4 1.1 %gather_fusion.4 = s32[128]{0:T(128)S(1)} fusion(s32[4096]{0:T(1024)S(1)} %copy-done, s32[1024]{0:T(1024)S(1)} %pad_clamp_fusion.4), kind=kCustom, calls=%fused_computation.clone | custom fusion | bytes 1536 | tf_op jit(solution)/shard_map/jit(_take)/gather | solution.py:244
  2.6 1.6 %gather_fusion.6 = s32[128]{0:T(128)S(1)} fusion(s32[4096]{0:T(1024)} %param.15, s32[1024]{0:T(1024)S(1)} %pad_clamp_fusion.4), kind=kCustom, calls=%fused_computation.2.clone | custom fusion | bytes 1536 | tf_op jit(solution)/shard_map/jit(_take)/gather | solution.py:244
  4.3 2.9 %copy.27 = f32[256,2048]{0,1:T(8,128)} copy(f32[256,2048]{1,0:T(8,128)} %param.12) | data formatting | bytes 4194304 | tf_op args[0]
  7.2 2.5 %gather_fusion.5 = f32[128,256]{1,0:T(8,128)S(1)} fusion(f32[256,2048]{0,1:T(8,128)} %copy.27, s32[1024]{0:T(1024)S(1)} %get-tuple-element.42), kind=kCustom, calls=%fused_computation.1.clone | custom fusion | bytes 262656 | tf_op jit(solution)/shard_map/jit(_take)/gather | solution.py:241
  9.7 0.0 copy-start.1
  9.7 0.1 copy.28
  9.8 2.3 %gather_fusion.7 = f32[128,256]{1,0:T(8,128)S(1)} fusion(f32[256,2048]{0,1:T(8,128)} %copy.27, s32[1024]{0:T(1024)S(1)} %get-tuple-element.41), kind=kCustom, calls=%fused_computation.3.clone | custom fusion | bytes 262656 | tf_op jit(solution)/shard_map/jit(_take)/gather | solution.py:241
  12.1 0.1 copy.30
  12.3 0.0 copy-done.4
  12.3 0.2 convert_reduce_fusion
  12.5 0.1 select_reduce_fusion.2
  12.7 0.1 reshape.292
  12.7 0.1 fusion.31
  12.9 0.0 copy-done.2
  12.9 0.6 gather_fusion
  13.5 0.1 reshape.207
  13.6 0.1 broadcast_select_fusion.1
  13.7 0.0 copy-done.1
  13.7 0.7 gather_fusion.1
  14.3 0.1 copy.34
  14.4 0.6 compare_reduce_fusion.4
  15.1 0.7 select_select_fusion.2
  15.7 0.1 fusion.30
  15.9 0.1 reshape.206
  16.0 0.1 fusion.8.rows_ref
  16.1 60.2 %shard_map.68 = (f32[256,128]{1,0:T(8,128)S(1)}, f32[16,16,2176]{2,1,0:T(8,128)S(1)}, f32[16,16,128]{2,1,0:T(8,128)S(1)}) custom-call(s32[16]{0:T(128)S(1)} %broadcast_select_fusion.3.pick_ref, f32[256,128]{1,0:T(8,128)S(1)} %fusion.9.x_ref, f32[16,2176]{1,0:T(8,128)S(1)} %fusion.8.rows_ref), custom_call_target="tpu_custom_call" | custom-call | tf_op jit(solution)/shard_map/pallas_call | solution.py:181
  76.3 0.1 add_add_fusion
  76.3 0.1 reshape.211
  76.4 0.6 gather_fusion.2
  77.1 0.1 reshape.205
  77.2 0.1 broadcast_select_fusion.2
  77.3 0.2 fusion.28
  77.5 0.1 copy.35
  77.6 5.8 %cholesky.44 = f32[64,64]{1,0:T(8,128)S(1)} custom-call(f32[64,64]{1,0:T(8,128)S(1)} %fusion.23), custom_call_target="Cholesky" | custom-call | tf_op jit(solution)/shard_map/jit(cholesky)/cholesky | solution.py:215
  83.5 0.6 compare_reduce_fusion.3
  84.1 0.7 fusion.12
  84.8 4.9 %custom-call.12 = f32[1,64,64]{1,2,0:T(8,128)S(1)} custom-call(f32[1,64,64]{2,1,0:T(8,128)S(1)} %fusion.12), custom_call_target="InvertDiagBlocksLowerTriangular" | custom-call | tf_op jit(solution)/shard_map/triangular_solve | solution.py:209
  89.7 0.3 fusion.4
  90.0 0.3 fusion.21
  90.3 0.2 fusion.19
  90.5 0.3 fusion.2
  90.8 0.2 fusion.37
  91.0 0.1 copy.36
  91.1 5.8 %cholesky.55 = f32[64,64]{1,0:T(8,128)S(1)} custom-call(f32[64,64]{1,0:T(8,128)S(1)} %fusion.18), custom_call_target="Cholesky" | custom-call | tf_op jit(solution)/shard_map/jit(cholesky)/cholesky | solution.py:215
  97.0 0.6 compare_reduce_fusion.2
  97.6 0.7 fusion.13
  98.3 4.9 %custom-call.13 = f32[1,64,64]{1,2,0:T(8,128)S(1)} custom-call(f32[1,64,64]{2,1,0:T(8,128)S(1)} %fusion.13), custom_call_target="InvertDiagBlocksLowerTriangular" | custom-call | tf_op jit(solution)/shard_map/triangular_solve | solution.py:209
  103.2 0.1 compare_reduce_fusion.1
  103.3 0.4 fusion.1
  103.7 0.3 fusion.38
  104.0 0.3 fusion.16
  104.3 0.2 fusion.14
  104.5 0.2 convolution_add_fusion.2
  104.7 1.1 gather_fusion.3
  105.8 0.0 copy-start.3
  105.8 0.1 broadcast_select_fusion
  105.9 0.1 slice_reduce_fusion
  106.0 0.2 fusion.10
  106.2 0.6 add_multiply_fusion
  106.8 0.6 copy-done.3
  107.4 3.2 %fusion = f32[256,2048]{1,0:T(8,128)} fusion(f32[256,2048]{1,0:T(8,128)S(1)} %copy-done.3, f32[128,2176]{1,0:T(8,128)S(1)} %broadcast_select_fusion, f32[256]{0:T(256)S(1)} %get-tuple-element.34, f32[256,64]{0,1:T(8,128)S(1)} %bitcast.60, f32[256,64]{0,1:T(8,128)S(1)} %convolution_add_fusion.2), kind=kOutput, calls=%fused_computation.9 | convolution fusion | flops 806387712 | bytes 5374976 | tf_op jit(solution)/shard_map/dot_general | solution.py:294
  (26 shorter events, 0.3 us)
Async XLA Ops:
  0.6 0.8 copy-start
  7.2 5.1 %copy-start.4 = (s32[2,64]{1,0:T(2,128)S(1)}, s32[2,64]{1,0:T(2,128)}, u32[]{:S(2)}) copy-start(s32[2,64]{1,0:T(2,128)} %param.16) | copy-start | bytes 1540
  7.2 5.7 %copy-start.2 = (f32[256,2048]{1,0:T(8,128)S(1)}, f32[256,2048]{1,0:T(8,128)}, u32[]{:S(2)}) copy-start(f32[256,2048]{1,0:T(8,128)} %param.12) | copy-start | bytes 6291460
  9.7 4.0 %copy-start.1 = (f32[256]{0:T(256)S(1)}, f32[256]{0:T(256)}, u32[]{:S(2)}) copy-start(f32[256]{0:T(256)} %param.13) | copy-start | bytes 3076
  105.8 1.6 %copy-start.3 = (f32[256,2048]{1,0:T(8,128)S(1)}, f32[256,2048]{1,0:T(8,128)}, u32[]{:S(2)}) copy-start(f32[256,2048]{1,0:T(8,128)} %param.12) | copy-start | bytes 6291460

commit v5 on v4

--- a/solution.py
+++ b/solution.py
@@ -44,7 +44,7 @@
 
 def _exchange_kernel(
     n_bus, n_line, pieces, pick_ref, x_ref, rows_ref, o_ref, o_rows, o_small,
-    recv, gathered, mine, held, picked, got, s1, r1, s2, r2, sr, rr, sl, rl, s3, r3,
+    recv, gathered, mine, held, picked, got, s1, r1, s2, r2, sr, rr, sl, rl, tsr, trr, tsl, trl,
 ):
     me = lax.axis_index("bus")
     here = lax.axis_index("line")
@@ -64,36 +64,55 @@
         )
         return carry
 
-    def greet_line(k, carry):
+    lax.fori_loop(1, n_bus, greet_bus, 0)
+    for neighbour in (left, right):
         pl.semaphore_signal(
-            barrier, 1, device_id=_mesh_id("line", lax.rem(here + k, n_line)),
-            device_id_type=mesh_type,
+            barrier, 1, device_id=_mesh_id("line", neighbour), device_id_type=mesh_type
         )
-        return carry
-
-    lax.fori_loop(1, n_bus, greet_bus, 0)
-    lax.fori_loop(1, n_line, greet_line, 0)
-    pl.semaphore_wait(barrier, n_bus - 1 + n_line - 1)
-
-    def ring(step, part, toward):
+    pl.semaphore_wait(barrier, n_bus - 1 + 2)
+
+    def ring_steps(toward):
+        return to_right if toward == "right" else to_left
+
+    def ring_copy(step, part, toward, first, buf, parts, sems):
+        send_right, recv_right, send_left, recv_left = sems
         if toward == "right":
             origin = lax.rem(here - (step - 1) + n_line, n_line)
-            peer, send_sem, recv_sem = right, sr, rr
+            peer, send_sem, recv_sem = right, send_right, recv_right
         else:
             origin = lax.rem(here + (step - 1), n_line)
-            peer, send_sem, recv_sem = left, sl, rl
-        rows = pl.ds(part * piece, piece)
-        src = rows_ref.at[rows] if step == 1 else held.at[origin, rows]
-        slot = (step - 1) * pieces + part
-        return _remote(src, held.at[origin, rows], send_sem.at[slot], recv_sem.at[slot], "line", peer)
-
-    def ring_steps(toward):
-        return to_right if toward == "right" else to_left
-
-    for part in range(pieces):
+            peer, send_sem, recv_sem = left, send_left, recv_left
+        size = first.shape[0] // parts
+        rows = pl.ds(part * size, size)
+        src = first.at[rows] if step == 1 else buf.at[origin, rows]
+        slot = (step - 1) * parts + part
+        return _remote(src, buf.at[origin, rows], send_sem.at[slot], recv_sem.at[slot], "line", peer)
+
+    def big(step):
+        return lambda part, toward: ring_copy(step, part, toward, rows_ref, held, pieces, (sr, rr, sl, rl))
+
+    def small(step):
+        return lambda part, toward: ring_copy(step, part, toward, picked, got, 1, (tsr, trr, tsl, trl))
+
+    def advance(copies, step, parts):
+        for part in range(parts):
+            for toward in ("right", "left"):
+                if step <= ring_steps(toward):
+                    if step > 1:
+                        copies(step - 1)(part, toward).wait_recv()
+                    copies(step)(part, toward).start()
+
+    def drain(copies, parts):
         for toward in ("right", "left"):
-            if ring_steps(toward) >= 1:
-                ring(1, part, toward).start()
+            last = ring_steps(toward)
+            for part in range(parts):
+                if last >= 1:
+                    copies(last)(part, toward).wait_recv()
+            for step in range(1, last + 1):
+                for part in range(parts):
+                    copies(step)(part, toward).wait_send()
+
+    advance(big, 1, pieces)
 
     def send1(k):
         peer = lax.rem(me + k, n_bus)
@@ -105,6 +124,7 @@
 
     lax.fori_loop(1, n_bus, start1, 0)
     held[here] = rows_ref[...]
+    advance(big, 2, pieces)
     total = x_ref[pl.ds(me * chunk, chunk), :]
 
     def finish1(k, acc):
@@ -124,13 +144,7 @@
         return carry
 
     lax.fori_loop(1, n_bus, start2, 0)
-
-    for step in range(2, to_right + 1):
-        for part in range(pieces):
-            for toward in ("right", "left"):
-                if step <= ring_steps(toward):
-                    ring(step - 1, part, toward).wait_recv()
-                    ring(step, part, toward).start()
+    advance(big, 3, pieces)
 
     def finish2(k, carry):
         send2(k).wait()
@@ -141,31 +155,16 @@
     for i in range(picked.shape[0]):
         picked[pl.ds(i, 1), :] = gathered[pl.ds(pick_ref[i], 1), :]
     got[here] = picked[...]
-
-    def send3(k):
-        peer = lax.rem(here + k, n_line)
-        return _remote(picked, got.at[here], s3.at[k], r3.at[k], "line", peer)
-
-    def start3(k, carry):
-        send3(k).start()
-        return carry
-
-    lax.fori_loop(1, n_line, start3, 0)
-
-    for toward in ("right", "left"):
-        last = ring_steps(toward)
-        for part in range(pieces):
-            if last >= 1:
-                ring(last, part, toward).wait_recv()
-        for step in range(1, last + 1):
-            for part in range(pieces):
-                ring(step, part, toward).wait_send()
-
-    def finish3(k, carry):
-        send3(k).wait()
-        return carry
-
-    lax.fori_loop(1, n_line, finish3, 0)
+    advance(small, 1, 1)
+    next_small = 2
+    for step in range(4, to_right + 1):
+        advance(big, step, pieces)
+        advance(small, next_small, 1)
+        next_small += 1
+    for step in range(next_small, to_right + 1):
+        advance(small, step, 1)
+    drain(big, pieces)
+    drain(small, 1)
     o_ref[...] = gathered[...]
     o_rows[...] = held[...]
     o_small[...] = got[...]
@@ -197,7 +196,7 @@
         ]
         + [pltpu.SemaphoreType.DMA((n_bus,))] * 4
         + [pltpu.SemaphoreType.DMA((n_line * pieces,))] * 4
-        + [pltpu.SemaphoreType.DMA((n_line,))] * 2,
+        + [pltpu.SemaphoreType.DMA((n_line,))] * 4,
         compiler_params=pltpu.CompilerParams(
             collective_id=0, has_side_effects=True, vmem_limit_bytes=48 * 1024 * 1024
         ),

time: 112 us -> 107 us (0.955)
  Pallas kernels: 60.2 us -> 54.9 us
    pallas_call x1, Pallas kernels: 60.2 us -> 54.9 us  [exchange(): pl.pallas_call(functools.partial(_exchange_kernel, n_bus, n_line, pieces)...]
where the time goes in v5:
time: 107 us; the launch traced here: 105 us
  Pallas kernels  54.9 us (51%)
  other arithmetic  27.4 us (26%)
  local copies, waits for them, and re-layouts  15.8 us (15%)
  matrix products  6.2 us (6%)
    pallas_call x1, Pallas kernels, exchange(): pl.pallas_call(functools.partial(_exchange_kernel, n_bus, n_line, pieces)...  54.9 us
    another operation x6, other arithmetic, solve_weights(): jnp.linalg.cholesky(jnp.dot(capacitance, capacitance.T, precision=PRECISE))  13 us
    another operation x4, other arithmetic, chol_solve(): lax.linalg.triangular_solve(factor_lower, middle, left_side=True, lower=T...  11.1 us
    gather x4, local copies, waits for them, and re-layouts, local_column(): jnp.take(transfer_factors, jnp.clip(offset, 0, local_cols - 1), axis=1)  5.02 us
    unnamed x11, local copies, waits for them, and re-layouts  3.48 us
    dot_general x1, matrix products, per_device(): jnp.dot(combined, outage_rows, precision=PRECISE)  3.24 us

profile of v5, /device:TPU:6, one launch (start us, length us, event | category | flops | bytes accessed | tf_op | source)
XLA Modules:
  0.0 105.3 jit_solution(18260064798774322962)
XLA Ops:
  0.6 0.0 copy-start
  0.6 0.8 reshape.208
  1.4 0.0 copy-done
  1.4 1.1 %gather_fusion.4 = s32[128]{0:T(128)S(1)} fusion(s32[4096]{0:T(1024)S(1)} %copy-done, s32[1024]{0:T(1024)S(1)} %pad_clamp_fusion.4), kind=kCustom, calls=%fused_computation.clone | custom fusion | bytes 1536 | tf_op jit(solution)/shard_map/jit(_take)/gather | solution.py:243
  2.6 1.6 %gather_fusion.6 = s32[128]{0:T(128)S(1)} fusion(s32[4096]{0:T(1024)} %param.15, s32[1024]{0:T(1024)S(1)} %pad_clamp_fusion.4), kind=kCustom, calls=%fused_computation.2.clone | custom fusion | bytes 1536 | tf_op jit(solution)/shard_map/jit(_take)/gather | solution.py:243
  4.3 2.9 %copy.27 = f32[256,2048]{0,1:T(8,128)} copy(f32[256,2048]{1,0:T(8,128)} %param.12) | data formatting | bytes 4194304 | tf_op args[0]
  7.2 2.5 %gather_fusion.5 = f32[128,256]{1,0:T(8,128)S(1)} fusion(f32[256,2048]{0,1:T(8,128)} %copy.27, s32[1024]{0:T(1024)S(1)} %get-tuple-element.42), kind=kCustom, calls=%fused_computation.1.clone | custom fusion | bytes 262656 | tf_op jit(solution)/shard_map/jit(_take)/gather | solution.py:240
  9.7 0.0 copy-start.1
  9.7 0.1 copy.28
  9.8 2.3 %gather_fusion.7 = f32[128,256]{1,0:T(8,128)S(1)} fusion(f32[256,2048]{0,1:T(8,128)} %copy.27, s32[1024]{0:T(1024)S(1)} %get-tuple-element.41), kind=kCustom, calls=%fused_computation.3.clone | custom fusion | bytes 262656 | tf_op jit(solution)/shard_map/jit(_take)/gather | solution.py:240
  12.1 0.1 copy.30
  12.3 0.0 copy-done.4
  12.3 0.2 convert_reduce_fusion
  12.5 0.1 select_reduce_fusion.2
  12.7 0.1 reshape.292
  12.7 0.1 fusion.31
  12.9 0.0 copy-done.2
  12.9 0.6 gather_fusion
  13.5 0.1 reshape.207
  13.6 0.1 broadcast_select_fusion.1
  13.7 0.0 copy-done.1
  13.7 0.7 gather_fusion.1
  14.3 0.1 copy.34
  14.4 0.6 compare_reduce_fusion.4
  15.1 0.7 select_select_fusion.2
  15.7 0.1 fusion.30
  15.9 0.1 reshape.206
  16.0 0.1 fusion.8.rows_ref
  16.1 54.9 %shard_map.68 = (f32[256,128]{1,0:T(8,128)S(1)}, f32[16,16,2176]{2,1,0:T(8,128)S(1)}, f32[16,16,128]{2,1,0:T(8,128)S(1)}) custom-call(s32[16]{0:T(128)S(1)} %broadcast_select_fusion.3.pick_ref, f32[256,128]{1,0:T(8,128)S(1)} %fusion.9.x_ref, f32[16,2176]{1,0:T(8,128)S(1)} %fusion.8.rows_ref), custom_call_target="tpu_custom_call" | custom-call | tf_op jit(solution)/shard_map/pallas_call | solution.py:180
  71.0 0.1 add_add_fusion
  71.0 0.1 reshape.211
  71.1 0.6 gather_fusion.2
  71.8 0.1 reshape.205
  71.9 0.1 broadcast_select_fusion.2
  72.0 0.2 fusion.28
  72.2 0.1 copy.35
  72.3 5.8 %cholesky.44 = f32[64,64]{1,0:T(8,128)S(1)} custom-call(f32[64,64]{1,0:T(8,128)S(1)} %fusion.23), custom_call_target="Cholesky" | custom-call | tf_op jit(solution)/shard_map/jit(cholesky)/cholesky | solution.py:214
  78.1 0.6 compare_reduce_fusion.3
  78.8 0.7 fusion.12
  79.5 4.9 %custom-call.12 = f32[1,64,64]{1,2,0:T(8,128)S(1)} custom-call(f32[1,64,64]{2,1,0:T(8,128)S(1)} %fusion.12), custom_call_target="InvertDiagBlocksLowerTriangular" | custom-call | tf_op jit(solution)/shard_map/triangular_solve | solution.py:208
  84.4 0.3 fusion.4
  84.7 0.3 fusion.21
  85.0 0.2 fusion.19
  85.2 0.3 fusion.2
  85.5 0.2 fusion.37
  85.7 0.1 copy.36
  85.8 5.8 %cholesky.55 = f32[64,64]{1,0:T(8,128)S(1)} custom-call(f32[64,64]{1,0:T(8,128)S(1)} %fusion.18), custom_call_target="Cholesky" | custom-call | tf_op jit(solution)/shard_map/jit(cholesky)/cholesky | solution.py:214
  91.6 0.6 compare_reduce_fusion.2
  92.3 0.7 fusion.13
  92.9 4.9 %custom-call.13 = f32[1,64,64]{1,2,0:T(8,128)S(1)} custom-call(f32[1,64,64]{2,1,0:T(8,128)S(1)} %fusion.13), custom_call_target="InvertDiagBlocksLowerTriangular" | custom-call | tf_op jit(solution)/shard_map/triangular_solve | solution.py:208
  97.9 0.1 compare_reduce_fusion.1
  98.0 0.4 fusion.1
  98.4 0.3 fusion.38
  98.7 0.3 fusion.16
  99.0 0.2 fusion.14
  99.2 0.2 convolution_add_fusion.2
  99.4 1.1 %gather_fusion.3 = f32[128,2176]{1,0:T(8,128)S(1)} fusion(f32[256,2176]{1,0:T(8,128)S(1)} %bitcast.56, s32[1024]{0:T(1024)S(1)} %pad_clamp_fusion), kind=kCustom, calls=%fused_computation.7 | custom fusion | bytes 2228736 | tf_op jit(solution)/shard_map/jit(_take)/gather | solution.py:263
  100.4 0.0 copy-start.3
  100.5 0.1 broadcast_select_fusion
  100.6 0.1 slice_reduce_fusion
  100.7 0.2 fusion.10
  100.9 0.6 add_multiply_fusion
  101.5 0.6 copy-done.3
  102.0 3.2 %fusion = f32[256,2048]{1,0:T(8,128)} fusion(f32[256,2048]{1,0:T(8,128)S(1)} %copy-done.3, f32[128,2176]{1,0:T(8,128)S(1)} %broadcast_select_fusion, f32[256]{0:T(256)S(1)} %get-tuple-element.34, f32[256,64]{0,1:T(8,128)S(1)} %bitcast.60, f32[256,64]{0,1:T(8,128)S(1)} %convolution_add_fusion.2), kind=kOutput, calls=%fused_computation.9 | convolution fusion | flops 806387712 | bytes 5374976 | tf_op jit(solution)/shard_map/dot_general | solution.py:293
  (26 shorter events, 0.3 us)
Async XLA Ops:
  0.6 0.8 copy-start
  7.2 5.1 %copy-start.4 = (s32[2,64]{1,0:T(2,128)S(1)}, s32[2,64]{1,0:T(2,128)}, u32[]{:S(2)}) copy-start(s32[2,64]{1,0:T(2,128)} %param.16) | copy-start | bytes 1540
  7.2 5.7 %copy-start.2 = (f32[256,2048]{1,0:T(8,128)S(1)}, f32[256,2048]{1,0:T(8,128)}, u32[]{:S(2)}) copy-start(f32[256,2048]{1,0:T(8,128)} %param.12) | copy-start | bytes 6291460
  9.7 4.0 %copy-start.1 = (f32[256]{0:T(256)S(1)}, f32[256]{0:T(256)}, u32[]{:S(2)}) copy-start(f32[256]{0:T(256)} %param.13) | copy-start | bytes 3076
  100.4 1.6 %copy-start.3 = (f32[256,2048]{1,0:T(8,128)S(1)}, f32[256,2048]{1,0:T(8,128)}, u32[]{:S(2)}) copy-start(f32[256,2048]{1,0:T(8,128)} %param.12) | copy-start | bytes 6291460

commit v6 on v5

--- a/solution.py
+++ b/solution.py
@@ -43,8 +43,9 @@
 
 
 def _exchange_kernel(
-    n_bus, n_line, pieces, pick_ref, x_ref, rows_ref, o_ref, o_rows, o_small,
-    recv, gathered, mine, held, picked, got, s1, r1, s2, r2, sr, rr, sl, rl, tsr, trr, tsl, trl,
+    n_bus, n_line, pieces, pick_ref, p_ref, ends_ref, rows_ref, o_ref, o_rows, o_small,
+    x_ref, recv, gathered, mine, held, picked, got, s1, r1, s2, r2, sr, rr, sl, rl,
+    tsr, trr, tsl, trl,
 ):
     me = lax.axis_index("bus")
     here = lax.axis_index("line")
@@ -113,6 +114,15 @@
                     copies(step)(part, toward).wait_send()
 
     advance(big, 1, pieces)
+
+    local_cols = p_ref.shape[1]
+    column = lax.broadcasted_iota(jnp.int32, (local_cols, ends_ref.shape[1]), 0)
+    select = (column == ends_ref[0:1, :]).astype(jnp.float32) - (
+        column == ends_ref[1:2, :]
+    ).astype(jnp.float32)
+    x_ref[...] = jnp.dot(
+        p_ref[...], select, precision=PRECISE, preferred_element_type=jnp.float32
+    )
 
     def send1(k):
         peer = lax.rem(me + k, n_bus)
@@ -170,7 +180,8 @@
     o_small[...] = got[...]
 
 
-def exchange(pick, x, rows, n_bus, n_line, pieces=2):
+def exchange(pick, factors, ends, rows, n_bus, n_line, pieces=2):
+    x = jax.ShapeDtypeStruct((factors.shape[0], ends.shape[1]), factors.dtype)
     x_rows, x_cols = x.shape
     chunk = x_rows // n_bus
     vmem = pl.BlockSpec(memory_space=pltpu.VMEM)
@@ -184,9 +195,10 @@
             jax.ShapeDtypeStruct(held_shape, rows.dtype),
             jax.ShapeDtypeStruct(got_shape, x.dtype),
         ),
-        in_specs=[smem, vmem, vmem],
+        in_specs=[smem, vmem, vmem, vmem],
         out_specs=(vmem, vmem, vmem),
         scratch_shapes=[
+            pltpu.VMEM(x.shape, x.dtype),
             pltpu.VMEM((n_bus, chunk, x_cols), x.dtype),
             pltpu.VMEM(x.shape, x.dtype),
             pltpu.VMEM((chunk, x_cols), x.dtype),
@@ -200,7 +212,7 @@
         compiler_params=pltpu.CompilerParams(
             collective_id=0, has_side_effects=True, vmem_limit_bytes=48 * 1024 * 1024
         ),
-    )(pick, x, rows)
+    )(pick, factors, ends, rows)
 
 
 def chol_solve(factor_lower, right):
@@ -236,11 +248,9 @@
 
     def local_column(bus):
         offset = bus - bus_index * local_cols
-        inside = (offset >= 0) & (offset < local_cols)
-        values = jnp.take(transfer_factors, jnp.clip(offset, 0, local_cols - 1), axis=1)
-        return jnp.where(inside[None, :], values, 0.0)
-
-    terminal_part = local_column(jnp.take(from_bus, ids)) - local_column(jnp.take(to_bus, ids))
+        return jnp.where((offset >= 0) & (offset < local_cols), offset, -1)
+
+    ends = jnp.stack([local_column(jnp.take(from_bus, ids)), local_column(jnp.take(to_bus, ids))])
 
     block, rank, slot = slot_layout(tripped, local_rows, cap)
     mine = (block == line_index)[:, None, :] & (
@@ -255,7 +265,7 @@
     rows = jnp.where(valid[:, None], jnp.concatenate([rows, extra], axis=1), 0.0)
     pick = jnp.where(valid, position, 0).astype(jnp.int32)
     terminal, gathered_rows, gathered_small = exchange(
-        pick, terminal_part, rows, lax.axis_size("bus"), lax.axis_size("line")
+        pick, transfer_factors, ends, rows, lax.axis_size("bus"), lax.axis_size("line")
     )
     gathered_rows = gathered_rows.reshape(-1, rows.shape[1])
     gathered_small = gathered_small.reshape(-1, terminal.shape[1])

time: 107 us -> 104 us (0.972)
  local copies, waits for them, and re-layouts: 15.8 us -> 9.96 us
  Pallas kernels: 54.9 us -> 56.6 us
  other arithmetic: 27.4 us -> 28.7 us
    gather x4 -> x0, local copies, waits for them, and re-layouts: 5.02 us -> none  [local_column(): jnp.take(transfer_factors, jnp.clip(offset, 0, local_cols - 1), axis=1)]
    pallas_call x1, Pallas kernels: 54.9 us -> 56.6 us  [exchange(): pl.pallas_call(functools.partial(_exchange_kernel, n_bus, n_line, pieces)...]
    gather x1, local copies, waits for them, and re-layouts: 0.6 us -> 2.26 us  [per_device(): rows = jnp.take(transfer_factors, position, axis=0)]
    unnamed x11 -> x12, local copies, waits for them, and re-layouts: 3.48 us -> 2.18 us
where the time goes in v6:
time: 104 us; the launch traced here: 102 us
  Pallas kernels  56.6 us (54%)
  other arithmetic  28.7 us (28%)
  local copies, waits for them, and re-layouts  9.96 us (10%)
  matrix products  6.2 us (6%)
    pallas_call x1, Pallas kernels, exchange(): pl.pallas_call(functools.partial(_exchange_kernel, n_bus, n_line, pieces)...  56.6 us
    another operation x6, other arithmetic, solve_weights(): jnp.linalg.cholesky(jnp.dot(capacitance, capacitance.T, precision=PRECISE))  13 us
    another operation x4, other arithmetic, chol_solve(): lax.linalg.triangular_solve(factor_lower, middle, left_side=True, lower=T...  11.1 us
    dot_general x1, matrix products, per_device(): jnp.dot(combined, outage_rows, precision=PRECISE)  3.24 us
    gather x1, local copies, waits for them, and re-layouts, per_device(): rows = jnp.take(transfer_factors, position, axis=0)  2.26 us
    unnamed x12, local copies, waits for them, and re-layouts  2.18 us

profile of v6, /device:TPU:6, one launch (start us, length us, event | category | flops | bytes accessed | tf_op | source)
XLA Modules:
  0.0 102.4 jit_solution(14687857758525854282)
XLA Ops:
  0.6 0.0 copy-start
  0.6 0.0 copy-start.3
  0.7 0.7 broadcast_compare_fusion
  1.4 0.2 convert_reduce_fusion
  1.6 0.7 broadcast_subtract_fusion
  2.2 0.1 select_reduce_fusion.2
  2.4 0.1 reshape.263
  2.5 0.1 fusion.30
  2.6 0.0 copy-start.5
  2.6 2.3 %gather_fusion = f32[16,2048]{1,0:T(8,128)S(1)} fusion(f32[256,2048]{1,0:T(8,128)} %p_ref.1, s32[1024]{0:T(1024)S(1)} %pad_clamp_fusion.1), kind=kCustom, calls=%fused_computation.2 | custom fusion | bytes 262208 | tf_op jit(solution)/shard_map/jit(_take)/gather | solution.py:262
  4.9 0.0 copy-start.4
  4.9 0.1 reshape.200
  5.0 0.1 broadcast_select_fusion.1
  5.1 0.0 copy-done.3
  5.1 0.7 gather_fusion.1
  5.7 0.1 copy.22
  5.8 0.6 compare_reduce_fusion.4
  6.5 0.7 select_select_fusion.2
  7.1 0.1 fusion.29
  7.3 0.1 reshape.199
  7.4 0.1 fusion.8.rows_ref
  7.5 0.0 copy-done.5
  7.5 0.1 reshape.201
  7.6 0.0 copy-done
  7.6 1.1 %gather_fusion.4 = s32[128]{0:T(128)S(1)} fusion(s32[4096]{0:T(1024)S(1)} %copy-done, s32[1024]{0:T(1024)S(1)} %pad_clamp_fusion.2), kind=kCustom, calls=%fused_computation.clone | custom fusion | bytes 1536 | tf_op jit(solution)/shard_map/jit(_take)/gather | solution.py:253
  8.8 1.1 %gather_fusion.5 = s32[128]{0:T(128)S(1)} fusion(s32[4096]{0:T(1024)S(1)} %copy-done.4, s32[1024]{0:T(1024)S(1)} %pad_clamp_fusion.2), kind=kCustom, calls=%fused_computation.1.clone | custom fusion | bytes 1536 | tf_op jit(solution)/shard_map/jit(_take)/gather | solution.py:253
  9.9 0.0 copy-start.1
  10.0 1.6 %copy-done.1 = f32[256,2048]{1,0:T(8,128)S(1)} copy-done((f32[256,2048]{1,0:T(8,128)S(1)}, f32[256,2048]{1,0:T(8,128)}, u32[]{:S(2)}) %copy-start.1) | copy-done | bytes 2097176
  11.5 56.6 %shard_map.68 = (f32[256,128]{1,0:T(8,128)S(1)}, f32[16,16,2176]{2,1,0:T(8,128)S(1)}, f32[16,16,128]{2,1,0:T(8,128)S(1)}) custom-call(s32[16]{0:T(128)S(1)} %broadcast_select_fusion.3.pick_ref, f32[256,2048]{1,0:T(8,128)S(1)} %copy-done.1, s32[2,128]{1,0:T(2,128)S(1)} %pad_add_fusion.ends_ref, f32[16,2176]{1,0:T(8,128)S(1)} %fusion.8.rows_ref), custom_call_target="tpu_custom_call" | custom-call | tf_op jit(solution)/shard_map/pallas_call | solution.py:191
  68.1 0.1 add_add_fusion
  68.2 0.1 reshape.204
  68.3 0.6 gather_fusion.2
  68.9 0.1 reshape.198
  69.0 0.1 broadcast_select_fusion.2
  69.1 0.2 fusion.27
  69.3 0.1 copy.23
  69.4 5.8 %cholesky.44 = f32[64,64]{1,0:T(8,128)S(1)} custom-call(f32[64,64]{1,0:T(8,128)S(1)} %fusion.22), custom_call_target="Cholesky" | custom-call | tf_op jit(solution)/shard_map/jit(cholesky)/cholesky | solution.py:226
  75.3 0.6 compare_reduce_fusion.3
  75.9 0.7 fusion.11
  76.6 4.9 %custom-call.12 = f32[1,64,64]{1,2,0:T(8,128)S(1)} custom-call(f32[1,64,64]{2,1,0:T(8,128)S(1)} %fusion.11), custom_call_target="InvertDiagBlocksLowerTriangular" | custom-call | tf_op jit(solution)/shard_map/triangular_solve | solution.py:220
  81.5 0.3 fusion.4
  81.8 0.3 fusion.20
  82.1 0.2 fusion.18
  82.4 0.3 fusion.2
  82.6 0.2 fusion.38
  82.8 0.1 copy.24
  82.9 5.8 %cholesky.55 = f32[64,64]{1,0:T(8,128)S(1)} custom-call(f32[64,64]{1,0:T(8,128)S(1)} %fusion.17), custom_call_target="Cholesky" | custom-call | tf_op jit(solution)/shard_map/jit(cholesky)/cholesky | solution.py:226
  88.8 0.6 compare_reduce_fusion.2
  89.4 0.7 fusion.12
  90.1 4.9 %custom-call.13 = f32[1,64,64]{1,2,0:T(8,128)S(1)} custom-call(f32[1,64,64]{2,1,0:T(8,128)S(1)} %fusion.12), custom_call_target="InvertDiagBlocksLowerTriangular" | custom-call | tf_op jit(solution)/shard_map/triangular_solve | solution.py:220
  95.0 0.1 compare_reduce_fusion.1
  95.1 0.4 fusion.1
  95.6 0.3 fusion.39
  95.8 0.3 fusion.15
  96.1 0.2 fusion.13
  96.3 0.2 convolution_add_fusion.2
  96.5 1.1 %gather_fusion.3 = f32[128,2176]{1,0:T(8,128)S(1)} fusion(f32[256,2176]{1,0:T(8,128)S(1)} %bitcast.52, s32[1024]{0:T(1024)S(1)} %pad_clamp_fusion), kind=kCustom, calls=%fused_computation.5 | custom fusion | bytes 2228736 | tf_op jit(solution)/shard_map/jit(_take)/gather | solution.py:273
  97.6 0.0 copy-start.2
  97.6 0.1 broadcast_select_fusion
  97.8 0.1 slice_reduce_fusion
  97.9 0.2 fusion.9
  98.0 0.6 add_multiply_fusion
  98.6 0.6 copy-done.2
  99.2 3.2 %fusion = f32[256,2048]{1,0:T(8,128)} fusion(f32[256,2048]{1,0:T(8,128)S(1)} %copy-done.2, f32[128,2176]{1,0:T(8,128)S(1)} %broadcast_select_fusion, f32[256]{0:T(256)S(1)} %get-tuple-element.27, f32[256,64]{0,1:T(8,128)S(1)} %bitcast.56, f32[256,64]{0,1:T(8,128)S(1)} %convolution_add_fusion.2), kind=kOutput, calls=%fused_computation.7 | convolution fusion | flops 806387712 | bytes 5374976 | tf_op jit(solution)/shard_map/dot_general | solution.py:303
  (21 shorter events, 0.2 us)
Async XLA Ops:
  0.6 7.0 %copy-start = (s32[4096]{0:T(1024)S(1)}, s32[4096]{0:T(1024)}, u32[]{:S(2)}) copy-start(s32[4096]{0:T(1024)} %param.12) | copy-start | bytes 49156
  0.6 4.4 %copy-start.3 = (f32[256]{0:T(256)S(1)}, f32[256]{0:T(256)}, u32[]{:S(2)}) copy-start(f32[256]{0:T(256)} %param.11) | copy-start | bytes 3076
  2.6 4.9 %copy-start.5 = (s32[2,64]{1,0:T(2,128)S(1)}, s32[2,64]{1,0:T(2,128)}, u32[]{:S(2)}) copy-start(s32[2,64]{1,0:T(2,128)} %param.14) | copy-start | bytes 1540
  4.9 3.9 %copy-start.4 = (s32[4096]{0:T(1024)S(1)}, s32[4096]{0:T(1024)}, u32[]{:S(2)}) copy-start(s32[4096]{0:T(1024)} %param.13) | copy-start | bytes 49156
  9.9 1.6 %copy-start.1 = (f32[256,2048]{1,0:T(8,128)S(1)}, f32[256,2048]{1,0:T(8,128)}, u32[]{:S(2)}) copy-start(f32[256,2048]{1,0:T(8,128)} %p_ref.1) | copy-start | bytes 6291460
  97.6 1.6 %copy-start.2 = (f32[256,2048]{1,0:T(8,128)S(1)}, f32[256,2048]{1,0:T(8,128)}, u32[]{:S(2)}) copy-start(f32[256,2048]{1,0:T(8,128)} %p_ref.1) | copy-start | bytes 6291460

commit v7 on v6

--- a/solution.py
+++ b/solution.py
@@ -43,7 +43,7 @@
 
 
 def _exchange_kernel(
-    n_bus, n_line, pieces, pick_ref, p_ref, ends_ref, rows_ref, o_ref, o_rows, o_small,
+    n_bus, n_line, pieces, pick_ref, p_ref, ends_ref, rows_ref, extra_ref, o_ref, o_rows, o_small,
     x_ref, recv, gathered, mine, held, picked, got, s1, r1, s2, r2, sr, rr, sl, rl,
     tsr, trr, tsl, trl,
 ):
@@ -162,8 +162,10 @@
 
     lax.fori_loop(1, n_bus, finish2, 0)
 
+    width = gathered.shape[1]
     for i in range(picked.shape[0]):
-        picked[pl.ds(i, 1), :] = gathered[pl.ds(pick_ref[i], 1), :]
+        picked[pl.ds(i, 1), :width] = gathered[pl.ds(pick_ref[i], 1), :]
+    picked[:, width:] = extra_ref[...]
     got[here] = picked[...]
     advance(small, 1, 1)
     next_small = 2
@@ -180,14 +182,14 @@
     o_small[...] = got[...]
 
 
-def exchange(pick, factors, ends, rows, n_bus, n_line, pieces=2):
+def exchange(pick, factors, ends, rows, extra, n_bus, n_line, pieces=4):
     x = jax.ShapeDtypeStruct((factors.shape[0], ends.shape[1]), factors.dtype)
     x_rows, x_cols = x.shape
     chunk = x_rows // n_bus
     vmem = pl.BlockSpec(memory_space=pltpu.VMEM)
     smem = pl.BlockSpec(memory_space=pltpu.SMEM)
     held_shape = (n_line,) + rows.shape
-    got_shape = (n_line, pick.shape[0], x_cols)
+    got_shape = (n_line, pick.shape[0], x_cols + extra.shape[1])
     return pl.pallas_call(
         functools.partial(_exchange_kernel, n_bus, n_line, pieces),
         out_shape=(
@@ -195,7 +197,7 @@
             jax.ShapeDtypeStruct(held_shape, rows.dtype),
             jax.ShapeDtypeStruct(got_shape, x.dtype),
         ),
-        in_specs=[smem, vmem, vmem, vmem],
+        in_specs=[smem, vmem, vmem, vmem, vmem],
         out_specs=(vmem, vmem, vmem),
         scratch_shapes=[
             pltpu.VMEM(x.shape, x.dtype),
@@ -203,7 +205,7 @@
             pltpu.VMEM(x.shape, x.dtype),
             pltpu.VMEM((chunk, x_cols), x.dtype),
             pltpu.VMEM(held_shape, rows.dtype),
-            pltpu.VMEM((pick.shape[0], x_cols), x.dtype),
+            pltpu.VMEM((pick.shape[0], x_cols + extra.shape[1]), x.dtype),
             pltpu.VMEM(got_shape, x.dtype),
         ]
         + [pltpu.SemaphoreType.DMA((n_bus,))] * 4
@@ -212,7 +214,7 @@
         compiler_params=pltpu.CompilerParams(
             collective_id=0, has_side_effects=True, vmem_limit_bytes=48 * 1024 * 1024
         ),
-    )(pick, factors, ends, rows)
+    )(pick, factors, ends, rows, extra)
 
 
 def chol_solve(factor_lower, right):
@@ -262,18 +264,18 @@
     rows = jnp.take(transfer_factors, position, axis=0)
     flows = jnp.take(line_flows, position)
     extra = jnp.zeros((position.shape[0], 128), jnp.float32).at[:, 0].set(flows)
-    rows = jnp.where(valid[:, None], jnp.concatenate([rows, extra], axis=1), 0.0)
+    rows = jnp.where(valid[:, None], rows, 0.0)
     pick = jnp.where(valid, position, 0).astype(jnp.int32)
     terminal, gathered_rows, gathered_small = exchange(
-        pick, transfer_factors, ends, rows, lax.axis_size("bus"), lax.axis_size("line")
+        pick, transfer_factors, ends, rows, extra, lax.axis_size("bus"), lax.axis_size("line")
     )
     gathered_rows = gathered_rows.reshape(-1, rows.shape[1])
-    gathered_small = gathered_small.reshape(-1, terminal.shape[1])
+    gathered_small = gathered_small.reshape(-1, gathered_small.shape[-1])
     slot_flat = slot.reshape(-1)
-    outage_all = jnp.take(gathered_rows, slot_flat, axis=0)
-    outage_rows = outage_all[:, :local_cols]
-    outage_flows = outage_all[:, local_cols]
-    outage_terms = jnp.take(gathered_small, slot_flat, axis=0)
+    outage_rows = jnp.take(gathered_rows, slot_flat, axis=0)
+    outage_small = jnp.take(gathered_small, slot_flat, axis=0)
+    outage_terms = outage_small[:, : terminal.shape[1]]
+    outage_flows = outage_small[:, terminal.shape[1]]
 
     identity = jnp.eye(outages, dtype=jnp.float32)
     row_global = line_index * local_rows + jnp.arange(local_rows, dtype=jnp.int32)

time: 104 us -> 105 us (level)
  matrix products: 6.2 us -> 7.83 us
    dot_general x1, matrix products: 3.24 us -> 4.87 us  [per_device(): jnp.dot(combined, outage_rows, precision=PRECISE)]
    unnamed x12 -> x10, local copies, waits for them, and re-layouts: 2.18 us -> 1.61 us
where the time goes in v7:
time: 105 us; the launch traced here: 104 us
  Pallas kernels  56.2 us (54%)
  other arithmetic  28.5 us (27%)
  local copies, waits for them, and re-layouts  10.1 us (10%)
  matrix products  7.83 us (7%)
    pallas_call x1, Pallas kernels, exchange(): pl.pallas_call(functools.partial(_exchange_kernel, n_bus, n_line, pieces)...  56.2 us
    another operation x6, other arithmetic, solve_weights(): jnp.linalg.cholesky(jnp.dot(capacitance, capacitance.T, precision=PRECISE))  13 us
    another operation x4, other arithmetic, chol_solve(): lax.linalg.triangular_solve(factor_lower, middle, left_side=True, lower=T...  11.1 us
    dot_general x1, matrix products, per_device(): jnp.dot(combined, outage_rows, precision=PRECISE)  4.87 us
    gather x1, local copies, waits for them, and re-layouts, per_device(): rows = jnp.take(transfer_factors, position, axis=0)  2.25 us

profile of v7, /device:TPU:6, one launch (start us, length us, event | category | flops | bytes accessed | tf_op | source)
XLA Modules:
  0.0 103.7 jit_solution(6765789753079015461)
XLA Ops:
  0.6 0.0 copy-start
  0.6 0.0 copy-start.4
  0.7 0.0 copy-start.3
  0.7 0.7 broadcast_compare_fusion
  1.4 0.2 convert_reduce_fusion
  1.6 0.7 broadcast_subtract_fusion
  2.3 0.1 select_reduce_fusion.2
  2.4 0.1 reshape.263
  2.5 0.1 fusion.31
  2.7 2.3 %gather_fusion = f32[16,2048]{1,0:T(8,128)S(1)} fusion(f32[256,2048]{1,0:T(8,128)} %p_ref.1, s32[1024]{0:T(1024)S(1)} %pad_clamp_fusion.1), kind=kCustom, calls=%fused_computation.2 | custom fusion | bytes 262208 | tf_op jit(solution)/shard_map/jit(_take)/gather | solution.py:264
  4.9 0.1 reshape.200
  5.0 0.1 fusion.30
  5.2 0.1 reshape.199
  5.2 0.1 select_select_fusion.rows_ref
  5.3 1.3 %gather_fusion.1 = f32[16]{0:T(128)S(1)} fusion(f32[256]{0:T(256)} %param.11, s32[1024]{0:T(1024)S(1)} %pad_clamp_fusion.1), kind=kCustom, calls=%fused_computation.3 | custom fusion | bytes 192 | tf_op jit(solution)/shard_map/jit(_take)/gather | solution.py:265
  6.7 0.1 copy.22
  6.8 0.6 compare_reduce_fusion.4
  7.4 0.7 select_select_fusion.3
  8.1 0.0 copy-done.4
  8.1 0.1 reshape.201
  8.2 0.0 copy-done
  8.2 1.1 %gather_fusion.4 = s32[128]{0:T(128)S(1)} fusion(s32[4096]{0:T(1024)S(1)} %copy-done, s32[1024]{0:T(1024)S(1)} %pad_clamp_fusion.2), kind=kCustom, calls=%fused_computation.clone | custom fusion | bytes 1536 | tf_op jit(solution)/shard_map/jit(_take)/gather | solution.py:255
  9.4 0.0 copy-done.3
  9.4 1.1 %gather_fusion.5 = s32[128]{0:T(128)S(1)} fusion(s32[4096]{0:T(1024)S(1)} %copy-done.3, s32[1024]{0:T(1024)S(1)} %pad_clamp_fusion.2), kind=kCustom, calls=%fused_computation.1.clone | custom fusion | bytes 1536 | tf_op jit(solution)/shard_map/jit(_take)/gather | solution.py:255
  10.6 0.0 copy-start.1
  10.6 1.6 %copy-done.1 = f32[256,2048]{1,0:T(8,128)S(1)} copy-done((f32[256,2048]{1,0:T(8,128)S(1)}, f32[256,2048]{1,0:T(8,128)}, u32[]{:S(2)}) %copy-start.1) | copy-done | bytes 2097176
  12.2 56.2 %shard_map.68 = (f32[256,128]{1,0:T(8,128)S(1)}, f32[16,16,2048]{2,1,0:T(8,128)S(1)}, f32[16,16,256]{2,1,0:T(8,128)S(1)}) custom-call(s32[16]{0:T(128)S(1)} %broadcast_select_fusion.1.pick_ref, f32[256,2048]{1,0:T(8,128)S(1)} %copy-done.1, s32[2,128]{1,0:T(2,128)S(1)} %pad_add_fusion.ends_ref, f32[16,2048]{1,0:T(8,128)S(1)} %select_select_fusion.rows_ref, ...), custom_call_target="tpu_custom_call" | custom-call | tf_op jit(solution)/shard_map/pallas_call | solution.py:193
  68.4 0.1 add_add_fusion
  68.5 0.1 reshape.204
  68.6 0.0 copy-start.2
  68.6 0.8 gather_fusion.2
  69.3 0.1 reshape.198
  69.4 0.1 broadcast_select_fusion
  69.5 0.2 fusion.28
  69.7 0.1 copy.23
  69.8 5.8 %cholesky.44 = f32[64,64]{1,0:T(8,128)S(1)} custom-call(f32[64,64]{1,0:T(8,128)S(1)} %fusion.23), custom_call_target="Cholesky" | custom-call | tf_op jit(solution)/shard_map/jit(cholesky)/cholesky | solution.py:228
  75.7 0.6 compare_reduce_fusion.3
  76.3 0.7 fusion.12
  77.0 4.9 %custom-call.12 = f32[1,64,64]{1,2,0:T(8,128)S(1)} custom-call(f32[1,64,64]{2,1,0:T(8,128)S(1)} %fusion.12), custom_call_target="InvertDiagBlocksLowerTriangular" | custom-call | tf_op jit(solution)/shard_map/triangular_solve | solution.py:222
  81.9 0.3 fusion.6
  82.2 0.3 fusion.21
  82.5 0.2 fusion.19
  82.8 0.3 fusion.2
  83.0 0.2 fusion.40
  83.2 0.1 copy.24
  83.3 5.8 %cholesky.55 = f32[64,64]{1,0:T(8,128)S(1)} custom-call(f32[64,64]{1,0:T(8,128)S(1)} %fusion.18), custom_call_target="Cholesky" | custom-call | tf_op jit(solution)/shard_map/jit(cholesky)/cholesky | solution.py:228
  89.2 0.6 compare_reduce_fusion.2
  89.8 0.7 fusion.13
  90.5 4.9 %custom-call.13 = f32[1,64,64]{1,2,0:T(8,128)S(1)} custom-call(f32[1,64,64]{2,1,0:T(8,128)S(1)} %fusion.13), custom_call_target="InvertDiagBlocksLowerTriangular" | custom-call | tf_op jit(solution)/shard_map/triangular_solve | solution.py:222
  95.4 0.1 compare_reduce_fusion.1
  95.6 0.4 fusion.1
  96.0 0.3 fusion.41
  96.3 0.3 fusion.16
  96.5 0.2 fusion.14
  96.7 0.2 convolution_add_fusion.2
  96.9 0.1 slice_reduce_fusion
  97.0 0.2 fusion.10
  97.2 0.0 copy-done.2
  97.2 0.6 add_multiply_fusion
  97.8 1.0 gather_fusion.3
  98.8 4.9 %fusion = f32[256,2048]{1,0:T(8,128)} fusion(f32[256,2048]{1,0:T(8,128)} %p_ref.1, f32[128,2048]{1,0:T(8,128)S(1)} %gather_fusion.3, f32[256]{0:T(256)S(1)} %get-tuple-element.27, pred[128]{0:T(512)(128)(4,1)S(1)} %compare_and_fusion.2, f32[256,64]{0,1:T(8,128)S(1)} %bitcast.56, f32[256,64]{0,1:T(8,128)S(1)} %convolution_add_fusion.2), kind=kOutput, calls=%fused_computation.7 | convolution fusion | flops 806649856 | bytes 5375104 | tf_op jit(solution)/shard_map/dot_general | solution.py:305
  (21 shorter events, 0.2 us)
Async XLA Ops:
  0.6 7.6 %copy-start = (s32[4096]{0:T(1024)S(1)}, s32[4096]{0:T(1024)}, u32[]{:S(2)}) copy-start(s32[4096]{0:T(1024)} %param.12) | copy-start | bytes 49156
  0.6 7.5 %copy-start.4 = (s32[2,64]{1,0:T(2,128)S(1)}, s32[2,64]{1,0:T(2,128)}, u32[]{:S(2)}) copy-start(s32[2,64]{1,0:T(2,128)} %param.14) | copy-start | bytes 1540
  0.7 8.7 %copy-start.3 = (s32[4096]{0:T(1024)S(1)}, s32[4096]{0:T(1024)}, u32[]{:S(2)}) copy-start(s32[4096]{0:T(1024)} %param.13) | copy-start | bytes 49156
  10.6 1.6 %copy-start.1 = (f32[256,2048]{1,0:T(8,128)S(1)}, f32[256,2048]{1,0:T(8,128)}, u32[]{:S(2)}) copy-start(f32[256,2048]{1,0:T(8,128)} %p_ref.1) | copy-start | bytes 6291460
  68.6 28.6 %copy-start.2 = (f32[256]{0:T(256)S(1)}, f32[256]{0:T(256)}, u32[]{:S(2)}) copy-start(f32[256]{0:T(256)} %param.11) | copy-start | bytes 3076

commit v8 on v7

--- a/solution.py
+++ b/solution.py
@@ -43,8 +43,8 @@
 
 
 def _exchange_kernel(
-    n_bus, n_line, pieces, pick_ref, p_ref, ends_ref, rows_ref, extra_ref, o_ref, o_rows, o_small,
-    x_ref, recv, gathered, mine, held, picked, got, s1, r1, s2, r2, sr, rr, sl, rl,
+    n_bus, n_line, pieces, pick_ref, p_ref, ends_ref, extra_ref, o_ref, o_rows, o_small,
+    rows_ref, x_ref, recv, gathered, mine, held, picked, got, s1, r1, s2, r2, sr, rr, sl, rl,
     tsr, trr, tsl, trl,
 ):
     me = lax.axis_index("bus")
@@ -113,6 +113,8 @@
                 for part in range(parts):
                     copies(step)(part, toward).wait_send()
 
+    for i in range(rows_ref.shape[0]):
+        rows_ref[pl.ds(i, 1), :] = p_ref[pl.ds(pick_ref[i], 1), :]
     advance(big, 1, pieces)
 
     local_cols = p_ref.shape[1]
@@ -182,7 +184,8 @@
     o_small[...] = got[...]
 
 
-def exchange(pick, factors, ends, rows, extra, n_bus, n_line, pieces=4):
+def exchange(pick, factors, ends, extra, n_bus, n_line, pieces=4):
+    rows = jax.ShapeDtypeStruct((pick.shape[0], factors.shape[1]), factors.dtype)
     x = jax.ShapeDtypeStruct((factors.shape[0], ends.shape[1]), factors.dtype)
     x_rows, x_cols = x.shape
     chunk = x_rows // n_bus
@@ -197,9 +200,10 @@
             jax.ShapeDtypeStruct(held_shape, rows.dtype),
             jax.ShapeDtypeStruct(got_shape, x.dtype),
         ),
-        in_specs=[smem, vmem, vmem, vmem, vmem],
+        in_specs=[smem, vmem, vmem, vmem],
         out_specs=(vmem, vmem, vmem),
         scratch_shapes=[
+            pltpu.VMEM(rows.shape, rows.dtype),
             pltpu.VMEM(x.shape, x.dtype),
             pltpu.VMEM((n_bus, chunk, x_cols), x.dtype),
             pltpu.VMEM(x.shape, x.dtype),
@@ -214,7 +218,7 @@
         compiler_params=pltpu.CompilerParams(
             collective_id=0, has_side_effects=True, vmem_limit_bytes=48 * 1024 * 1024
         ),
-    )(pick, factors, ends, rows, extra)
+    )(pick, factors, ends, extra)
 
 
 def chol_solve(factor_lower, right):
@@ -261,15 +265,13 @@
     position = jnp.sum(jnp.where(mine, (tripped - line_index * local_rows)[:, None, :], 0), axis=2)
     valid = jnp.any(mine, axis=2).reshape(-1)
     position = position.reshape(-1)
-    rows = jnp.take(transfer_factors, position, axis=0)
     flows = jnp.take(line_flows, position)
     extra = jnp.zeros((position.shape[0], 128), jnp.float32).at[:, 0].set(flows)
-    rows = jnp.where(valid[:, None], rows, 0.0)
     pick = jnp.where(valid, position, 0).astype(jnp.int32)
     terminal, gathered_rows, gathered_small = exchange(
-        pick, transfer_factors, ends, rows, extra, lax.axis_size("bus"), lax.axis_size("line")
-    )
-    gathered_rows = gathered_rows.reshape(-1, rows.shape[1])
+        pick, transfer_factors, ends, extra, lax.axis_size("bus"), lax.axis_size("line")
+    )
+    gathered_rows = gathered_rows.reshape(-1, local_cols)
     gathered_small = gathered_small.reshape(-1, gathered_small.shape[-1])
     slot_flat = slot.reshape(-1)
     outage_rows = jnp.take(gathered_rows, slot_flat, axis=0)

time: 105 us -> 104 us (level)
  local copies, waits for them, and re-layouts: 10.1 us -> 8.93 us
    gather x1 -> x0, local copies, waits for them, and re-layouts: 2.25 us -> none  [per_device(): rows = jnp.take(transfer_factors, position, axis=0)]
where the time goes in v8:
time: 104 us; the launch traced here: 102 us
  Pallas kernels  56.4 us (54%)
  other arithmetic  28.4 us (27%)
  local copies, waits for them, and re-layouts  8.93 us (9%)
  matrix products  7.82 us (8%)
    pallas_call x1, Pallas kernels, exchange(): pl.pallas_call(functools.partial(_exchange_kernel, n_bus, n_line, pieces)...  56.4 us
    another operation x6, other arithmetic, solve_weights(): jnp.linalg.cholesky(jnp.dot(capacitance, capacitance.T, precision=PRECISE))  13 us
    another operation x4, other arithmetic, chol_solve(): lax.linalg.triangular_solve(factor_lower, middle, left_side=True, lower=T...  11.1 us
    dot_general x1, matrix products, per_device(): jnp.dot(combined, outage_rows, precision=PRECISE)  4.87 us

profile of v8, /device:TPU:6, one launch (start us, length us, event | category | flops | bytes accessed | tf_op | source)
XLA Modules:
  0.0 102.5 jit_solution(10248166085594002978)
XLA Ops:
  0.6 0.0 copy-start
  0.7 0.7 broadcast_compare_fusion
  1.4 0.2 convert_reduce_fusion
  1.5 0.7 broadcast_subtract_fusion
  2.2 0.1 select_reduce_fusion.2
  2.4 0.1 reshape.250
  2.5 0.1 fusion.31
  2.6 1.3 %gather_fusion = f32[16]{0:T(128)S(1)} fusion(f32[256]{0:T(256)} %param.11, s32[1024]{0:T(1024)S(1)} %pad_clamp_fusion.1), kind=kCustom, calls=%fused_computation.2 | custom fusion | bytes 192 | tf_op jit(solution)/shard_map/jit(_take)/gather | solution.py:268
  3.9 0.1 copy.22
  4.0 0.6 compare_reduce_fusion.4
  4.7 0.7 select_select_fusion.2
  5.3 0.1 fusion.30
  5.5 0.1 select_n.87.pick_ref
  5.6 0.8 reshape.196
  6.4 0.0 copy-done
  6.4 1.1 %gather_fusion.3 = s32[128]{0:T(128)S(1)} fusion(s32[4096]{0:T(1024)S(1)} %copy-done, s32[1024]{0:T(1024)S(1)} %pad_clamp_fusion.2), kind=kCustom, calls=%fused_computation.clone | custom fusion | bytes 1536 | tf_op jit(solution)/shard_map/jit(_take)/gather | solution.py:259
  7.5 1.6 %gather_fusion.4 = s32[128]{0:T(128)S(1)} fusion(s32[4096]{0:T(1024)} %param.13, s32[1024]{0:T(1024)S(1)} %pad_clamp_fusion.2), kind=kCustom, calls=%fused_computation.1.clone | custom fusion | bytes 1536 | tf_op jit(solution)/shard_map/jit(_take)/gather | solution.py:259
  9.2 0.0 copy-start.1
  9.2 1.6 %copy-done.1 = f32[256,2048]{1,0:T(8,128)S(1)} copy-done((f32[256,2048]{1,0:T(8,128)S(1)}, f32[256,2048]{1,0:T(8,128)}, u32[]{:S(2)}) %copy-start.1) | copy-done | bytes 2097176
  10.8 0.0 copy-start.3
  10.8 56.4 %shard_map.68 = (f32[256,128]{1,0:T(8,128)S(1)}, f32[16,16,2048]{2,1,0:T(8,128)S(1)}, f32[16,16,256]{2,1,0:T(8,128)S(1)}) custom-call(s32[16]{0:T(128)S(1)} %select_n.87.pick_ref, f32[256,2048]{1,0:T(8,128)S(1)} %copy-done.1, s32[2,128]{1,0:T(2,128)S(1)} %pad_add_fusion.ends_ref, f32[16,128]{1,0:T(8,128)S(1)} %scatter.4.extra_ref), custom_call_target="tpu_custom_call" | custom-call | tf_op jit(solution)/shard_map/pallas_call | solution.py:196
  67.2 0.1 add_add_fusion
  67.3 0.1 reshape.199
  67.4 0.0 copy-start.2
  67.4 0.8 gather_fusion.1
  68.2 0.1 reshape.195
  68.3 0.1 broadcast_select_fusion
  68.4 0.2 fusion.28
  68.6 0.1 copy.23
  68.7 5.8 %cholesky.44 = f32[64,64]{1,0:T(8,128)S(1)} custom-call(f32[64,64]{1,0:T(8,128)S(1)} %fusion.23), custom_call_target="Cholesky" | custom-call | tf_op jit(solution)/shard_map/jit(cholesky)/cholesky | solution.py:232
  74.5 0.6 compare_reduce_fusion.3
  75.2 0.7 fusion.12
  75.8 4.9 %custom-call.12 = f32[1,64,64]{1,2,0:T(8,128)S(1)} custom-call(f32[1,64,64]{2,1,0:T(8,128)S(1)} %fusion.12), custom_call_target="InvertDiagBlocksLowerTriangular" | custom-call | tf_op jit(solution)/shard_map/triangular_solve | solution.py:226
  80.8 0.3 fusion.6
  81.1 0.3 fusion.21
  81.4 0.2 fusion.19
  81.6 0.3 fusion.2
  81.9 0.2 fusion.40
  82.1 0.1 copy.24
  82.2 5.8 %cholesky.55 = f32[64,64]{1,0:T(8,128)S(1)} custom-call(f32[64,64]{1,0:T(8,128)S(1)} %fusion.18), custom_call_target="Cholesky" | custom-call | tf_op jit(solution)/shard_map/jit(cholesky)/cholesky | solution.py:232
  88.0 0.6 compare_reduce_fusion.2
  88.7 0.7 fusion.13
  89.3 4.9 %custom-call.13 = f32[1,64,64]{1,2,0:T(8,128)S(1)} custom-call(f32[1,64,64]{2,1,0:T(8,128)S(1)} %fusion.13), custom_call_target="InvertDiagBlocksLowerTriangular" | custom-call | tf_op jit(solution)/shard_map/triangular_solve | solution.py:226
  94.3 0.0 copy-done.3
  94.3 0.1 compare_reduce_fusion.1
  94.4 0.4 fusion.1
  94.8 0.3 fusion.41
  95.1 0.3 fusion.16
  95.4 0.2 fusion.14
  95.6 0.2 convolution_add_fusion.2
  95.8 0.1 slice_reduce_fusion
  95.9 0.2 fusion.10
  96.1 0.0 copy-done.2
  96.1 0.6 add_multiply_fusion
  96.6 1.0 gather_fusion.2
  97.6 4.9 %fusion = f32[256,2048]{1,0:T(8,128)} fusion(f32[256,2048]{1,0:T(8,128)} %p_ref.1, f32[128,2048]{1,0:T(8,128)S(1)} %gather_fusion.2, f32[256]{0:T(256)S(1)} %get-tuple-element.27, pred[128]{0:T(512)(128)(4,1)S(1)} %compare_and_fusion.1, f32[256,64]{0,1:T(8,128)S(1)} %bitcast.56, f32[256,64]{0,1:T(8,128)S(1)} %convolution_add_fusion.2), kind=kOutput, calls=%fused_computation.6 | convolution fusion | flops 806649856 | bytes 5375104 | tf_op jit(solution)/shard_map/dot_general | solution.py:307
  (20 shorter events, 0.2 us)
Async XLA Ops:
  0.6 5.7 %copy-start = (s32[4096]{0:T(1024)S(1)}, s32[4096]{0:T(1024)}, u32[]{:S(2)}) copy-start(s32[4096]{0:T(1024)} %param.12) | copy-start | bytes 49156
  9.2 1.6 %copy-start.1 = (f32[256,2048]{1,0:T(8,128)S(1)}, f32[256,2048]{1,0:T(8,128)}, u32[]{:S(2)}) copy-start(f32[256,2048]{1,0:T(8,128)} %p_ref.1) | copy-start | bytes 6291460
  10.8 83.5 %copy-start.3 = (s32[2,64]{1,0:T(2,128)S(1)}, s32[2,64]{1,0:T(2,128)}, u32[]{:S(2)}) copy-start(s32[2,64]{1,0:T(2,128)} %param.14) | copy-start | bytes 1540
  67.4 28.6 %copy-start.2 = (f32[256]{0:T(256)S(1)}, f32[256]{0:T(256)}, u32[]{:S(2)}) copy-start(f32[256]{0:T(256)} %param.11) | copy-start | bytes 3076

commit v9 on v6

--- a/solution.py
+++ b/solution.py
@@ -169,8 +169,10 @@
     next_small = 2
     for step in range(4, to_right + 1):
         advance(big, step, pieces)
-        advance(small, next_small, 1)
-        next_small += 1
+        for _ in range(2):
+            if next_small <= to_right:
+                advance(small, next_small, 1)
+                next_small += 1
     for step in range(next_small, to_right + 1):
         advance(small, step, 1)
     drain(big, pieces)

time: 104 us -> 102 us (0.981)
  Pallas kernels: 56.6 us -> 54.6 us
    pallas_call x1, Pallas kernels: 56.6 us -> 54.6 us  [exchange(): pl.pallas_call(functools.partial(_exchange_kernel, n_bus, n_line, pieces)...]
where the time goes in v9:
time: 102 us; the launch traced here: 100 us
  Pallas kernels  54.6 us (54%)
  other arithmetic  28.7 us (28%)
  local copies, waits for them, and re-layouts  9.96 us (10%)
  matrix products  6.2 us (6%)
    pallas_call x1, Pallas kernels, exchange(): pl.pallas_call(functools.partial(_exchange_kernel, n_bus, n_line, pieces)...  54.6 us
    another operation x6, other arithmetic, solve_weights(): jnp.linalg.cholesky(jnp.dot(capacitance, capacitance.T, precision=PRECISE))  13 us
    another operation x4, other arithmetic, chol_solve(): lax.linalg.triangular_solve(factor_lower, middle, left_side=True, lower=T...  11.1 us
    dot_general x1, matrix products, per_device(): jnp.dot(combined, outage_rows, precision=PRECISE)  3.24 us
    gather x1, local copies, waits for them, and re-layouts, per_device(): rows = jnp.take(transfer_factors, position, axis=0)  2.26 us
    unnamed x12, local copies, waits for them, and re-layouts  2.18 us

profile of v9, /device:TPU:6, one launch (start us, length us, event | category | flops | bytes accessed | tf_op | source)
XLA Modules:
  0.0 100.4 jit_solution(12507741470635426713)
XLA Ops:
  0.6 0.0 copy-start
  0.6 0.0 copy-start.3
  0.7 0.7 broadcast_compare_fusion
  1.4 0.2 convert_reduce_fusion
  1.6 0.7 broadcast_subtract_fusion
  2.2 0.1 select_reduce_fusion.2
  2.4 0.1 reshape.263
  2.5 0.1 fusion.30
  2.6 0.0 copy-start.5
  2.6 2.3 %gather_fusion = f32[16,2048]{1,0:T(8,128)S(1)} fusion(f32[256,2048]{1,0:T(8,128)} %p_ref.1, s32[1024]{0:T(1024)S(1)} %pad_clamp_fusion.1), kind=kCustom, calls=%fused_computation.2 | custom fusion | bytes 262208 | tf_op jit(solution)/shard_map/jit(_take)/gather | solution.py:264
  4.9 0.0 copy-start.4
  4.9 0.1 reshape.200
  5.0 0.1 broadcast_select_fusion.1
  5.1 0.0 copy-done.3
  5.1 0.7 gather_fusion.1
  5.7 0.1 copy.22
  5.8 0.6 compare_reduce_fusion.4
  6.5 0.7 select_select_fusion.2
  7.1 0.1 fusion.29
  7.3 0.1 reshape.199
  7.4 0.1 fusion.8.rows_ref
  7.5 0.0 copy-done.5
  7.5 0.1 reshape.201
  7.6 1.1 %gather_fusion.4 = s32[128]{0:T(128)S(1)} fusion(s32[4096]{0:T(1024)S(1)} %copy-done, s32[1024]{0:T(1024)S(1)} %pad_clamp_fusion.2), kind=kCustom, calls=%fused_computation.clone | custom fusion | bytes 1536 | tf_op jit(solution)/shard_map/jit(_take)/gather | solution.py:255
  8.7 0.0 copy-done.4
  8.8 1.1 %gather_fusion.5 = s32[128]{0:T(128)S(1)} fusion(s32[4096]{0:T(1024)S(1)} %copy-done.4, s32[1024]{0:T(1024)S(1)} %pad_clamp_fusion.2), kind=kCustom, calls=%fused_computation.1.clone | custom fusion | bytes 1536 | tf_op jit(solution)/shard_map/jit(_take)/gather | solution.py:255
  9.9 0.0 copy-start.1
  10.0 1.6 %copy-done.1 = f32[256,2048]{1,0:T(8,128)S(1)} copy-done((f32[256,2048]{1,0:T(8,128)S(1)}, f32[256,2048]{1,0:T(8,128)}, u32[]{:S(2)}) %copy-start.1) | copy-done | bytes 2097176
  11.5 54.6 %shard_map.68 = (f32[256,128]{1,0:T(8,128)S(1)}, f32[16,16,2176]{2,1,0:T(8,128)S(1)}, f32[16,16,128]{2,1,0:T(8,128)S(1)}) custom-call(s32[16]{0:T(128)S(1)} %broadcast_select_fusion.3.pick_ref, f32[256,2048]{1,0:T(8,128)S(1)} %copy-done.1, s32[2,128]{1,0:T(2,128)S(1)} %pad_add_fusion.ends_ref, f32[16,2176]{1,0:T(8,128)S(1)} %fusion.8.rows_ref), custom_call_target="tpu_custom_call" | custom-call | tf_op jit(solution)/shard_map/pallas_call | solution.py:193
  66.1 0.1 add_add_fusion
  66.2 0.1 reshape.204
  66.3 0.6 gather_fusion.2
  66.9 0.1 reshape.198
  67.0 0.1 broadcast_select_fusion.2
  67.1 0.2 fusion.27
  67.3 0.1 copy.23
  67.4 5.8 %cholesky.44 = f32[64,64]{1,0:T(8,128)S(1)} custom-call(f32[64,64]{1,0:T(8,128)S(1)} %fusion.22), custom_call_target="Cholesky" | custom-call | tf_op jit(solution)/shard_map/jit(cholesky)/cholesky | solution.py:228
  73.3 0.6 compare_reduce_fusion.3
  73.9 0.7 fusion.11
  74.6 4.9 %custom-call.12 = f32[1,64,64]{1,2,0:T(8,128)S(1)} custom-call(f32[1,64,64]{2,1,0:T(8,128)S(1)} %fusion.11), custom_call_target="InvertDiagBlocksLowerTriangular" | custom-call | tf_op jit(solution)/shard_map/triangular_solve | solution.py:222
  79.5 0.3 fusion.4
  79.8 0.3 fusion.20
  80.1 0.2 fusion.18
  80.3 0.3 fusion.2
  80.6 0.2 fusion.38
  80.8 0.1 copy.24
  80.9 5.8 %cholesky.55 = f32[64,64]{1,0:T(8,128)S(1)} custom-call(f32[64,64]{1,0:T(8,128)S(1)} %fusion.17), custom_call_target="Cholesky" | custom-call | tf_op jit(solution)/shard_map/jit(cholesky)/cholesky | solution.py:228
  86.8 0.6 compare_reduce_fusion.2
  87.4 0.7 fusion.12
  88.1 4.9 %custom-call.13 = f32[1,64,64]{1,2,0:T(8,128)S(1)} custom-call(f32[1,64,64]{2,1,0:T(8,128)S(1)} %fusion.12), custom_call_target="InvertDiagBlocksLowerTriangular" | custom-call | tf_op jit(solution)/shard_map/triangular_solve | solution.py:222
  93.0 0.1 compare_reduce_fusion.1
  93.1 0.4 fusion.1
  93.6 0.3 fusion.39
  93.8 0.3 fusion.15
  94.1 0.2 fusion.13
  94.3 0.2 convolution_add_fusion.2
  94.5 1.1 %gather_fusion.3 = f32[128,2176]{1,0:T(8,128)S(1)} fusion(f32[256,2176]{1,0:T(8,128)S(1)} %bitcast.52, s32[1024]{0:T(1024)S(1)} %pad_clamp_fusion), kind=kCustom, calls=%fused_computation.5 | custom fusion | bytes 2228736 | tf_op jit(solution)/shard_map/jit(_take)/gather | solution.py:275
  95.6 0.0 copy-start.2
  95.6 0.1 broadcast_select_fusion
  95.7 0.1 slice_reduce_fusion
  95.9 0.2 fusion.9
  96.0 0.6 add_multiply_fusion
  96.6 0.6 copy-done.2
  97.2 3.2 %fusion = f32[256,2048]{1,0:T(8,128)} fusion(f32[256,2048]{1,0:T(8,128)S(1)} %copy-done.2, f32[128,2176]{1,0:T(8,128)S(1)} %broadcast_select_fusion, f32[256]{0:T(256)S(1)} %get-tuple-element.27, f32[256,64]{0,1:T(8,128)S(1)} %bitcast.56, f32[256,64]{0,1:T(8,128)S(1)} %convolution_add_fusion.2), kind=kOutput, calls=%fused_computation.7 | convolution fusion | flops 806387712 | bytes 5374976 | tf_op jit(solution)/shard_map/dot_general | solution.py:305
  (21 shorter events, 0.2 us)
Async XLA Ops:
  0.6 7.0 %copy-start = (s32[4096]{0:T(1024)S(1)}, s32[4096]{0:T(1024)}, u32[]{:S(2)}) copy-start(s32[4096]{0:T(1024)} %param.12) | copy-start | bytes 49156
  0.6 4.4 %copy-start.3 = (f32[256]{0:T(256)S(1)}, f32[256]{0:T(256)}, u32[]{:S(2)}) copy-start(f32[256]{0:T(256)} %param.11) | copy-start | bytes 3076
  2.6 4.9 %copy-start.5 = (s32[2,64]{1,0:T(2,128)S(1)}, s32[2,64]{1,0:T(2,128)}, u32[]{:S(2)}) copy-start(s32[2,64]{1,0:T(2,128)} %param.14) | copy-start | bytes 1540
  4.9 3.9 %copy-start.4 = (s32[4096]{0:T(1024)S(1)}, s32[4096]{0:T(1024)}, u32[]{:S(2)}) copy-start(s32[4096]{0:T(1024)} %param.13) | copy-start | bytes 49156
  9.9 1.6 %copy-start.1 = (f32[256,2048]{1,0:T(8,128)S(1)}, f32[256,2048]{1,0:T(8,128)}, u32[]{:S(2)}) copy-start(f32[256,2048]{1,0:T(8,128)} %p_ref.1) | copy-start | bytes 6291460
  95.6 1.6 %copy-start.2 = (f32[256,2048]{1,0:T(8,128)S(1)}, f32[256,2048]{1,0:T(8,128)}, u32[]{:S(2)}) copy-start(f32[256,2048]{1,0:T(8,128)} %p_ref.1) | copy-start | bytes 6291460

commit v10 on v9

--- a/solution.py
+++ b/solution.py
@@ -169,7 +169,7 @@
     next_small = 2
     for step in range(4, to_right + 1):
         advance(big, step, pieces)
-        for _ in range(2):
+        for _ in range(1 if step == 4 else 2):
             if next_small <= to_right:
                 advance(small, next_small, 1)
                 next_small += 1

time: 102 us -> 102 us (level)
  no operation moved by 1% of the time
where the time goes in v10:
time: 102 us; the launch traced here: 100 us
  Pallas kernels  54.6 us (54%)
  other arithmetic  28.7 us (28%)
  local copies, waits for them, and re-layouts  9.96 us (10%)
  matrix products  6.2 us (6%)
    pallas_call x1, Pallas kernels, exchange(): pl.pallas_call(functools.partial(_exchange_kernel, n_bus, n_line, pieces)...  54.6 us
    another operation x6, other arithmetic, solve_weights(): jnp.linalg.cholesky(jnp.dot(capacitance, capacitance.T, precision=PRECISE))  13 us
    another operation x4, other arithmetic, chol_solve(): lax.linalg.triangular_solve(factor_lower, middle, left_side=True, lower=T...  11.1 us
    dot_general x1, matrix products, per_device(): jnp.dot(combined, outage_rows, precision=PRECISE)  3.24 us
    gather x1, local copies, waits for them, and re-layouts, per_device(): rows = jnp.take(transfer_factors, position, axis=0)  2.26 us
    unnamed x12, local copies, waits for them, and re-layouts  2.18 us

profile of v10, /device:TPU:6, one launch (start us, length us, event | category | flops | bytes accessed | tf_op | source)
XLA Modules:
  0.0 100.5 jit_solution(9119043944295163020)
XLA Ops:
  0.6 0.0 copy-start
  0.6 0.0 copy-start.3
  0.7 0.7 broadcast_compare_fusion
  1.4 0.2 convert_reduce_fusion
  1.6 0.7 broadcast_subtract_fusion
  2.2 0.1 select_reduce_fusion.2
  2.4 0.1 reshape.263
  2.5 0.1 fusion.30
  2.6 0.0 copy-start.5
  2.6 2.3 %gather_fusion = f32[16,2048]{1,0:T(8,128)S(1)} fusion(f32[256,2048]{1,0:T(8,128)} %p_ref.1, s32[1024]{0:T(1024)S(1)} %pad_clamp_fusion.1), kind=kCustom, calls=%fused_computation.2 | custom fusion | bytes 262208 | tf_op jit(solution)/shard_map/jit(_take)/gather | solution.py:264
  4.9 0.0 copy-start.4
  4.9 0.1 reshape.200
  5.0 0.1 broadcast_select_fusion.1
  5.1 0.0 copy-done.3
  5.1 0.7 gather_fusion.1
  5.7 0.1 copy.22
  5.8 0.6 compare_reduce_fusion.4
  6.5 0.7 select_select_fusion.2
  7.1 0.1 fusion.29
  7.3 0.1 reshape.199
  7.4 0.1 fusion.8.rows_ref
  7.5 0.0 copy-done.5
  7.5 0.1 reshape.201
  7.6 1.1 %gather_fusion.4 = s32[128]{0:T(128)S(1)} fusion(s32[4096]{0:T(1024)S(1)} %copy-done, s32[1024]{0:T(1024)S(1)} %pad_clamp_fusion.2), kind=kCustom, calls=%fused_computation.clone | custom fusion | bytes 1536 | tf_op jit(solution)/shard_map/jit(_take)/gather | solution.py:255
  8.7 0.0 copy-done.4
  8.8 1.1 %gather_fusion.5 = s32[128]{0:T(128)S(1)} fusion(s32[4096]{0:T(1024)S(1)} %copy-done.4, s32[1024]{0:T(1024)S(1)} %pad_clamp_fusion.2), kind=kCustom, calls=%fused_computation.1.clone | custom fusion | bytes 1536 | tf_op jit(solution)/shard_map/jit(_take)/gather | solution.py:255
  9.9 0.0 copy-start.1
  10.0 1.6 %copy-done.1 = f32[256,2048]{1,0:T(8,128)S(1)} copy-done((f32[256,2048]{1,0:T(8,128)S(1)}, f32[256,2048]{1,0:T(8,128)}, u32[]{:S(2)}) %copy-start.1) | copy-done | bytes 2097176
  11.5 54.6 %shard_map.68 = (f32[256,128]{1,0:T(8,128)S(1)}, f32[16,16,2176]{2,1,0:T(8,128)S(1)}, f32[16,16,128]{2,1,0:T(8,128)S(1)}) custom-call(s32[16]{0:T(128)S(1)} %broadcast_select_fusion.3.pick_ref, f32[256,2048]{1,0:T(8,128)S(1)} %copy-done.1, s32[2,128]{1,0:T(2,128)S(1)} %pad_add_fusion.ends_ref, f32[16,2176]{1,0:T(8,128)S(1)} %fusion.8.rows_ref), custom_call_target="tpu_custom_call" | custom-call | tf_op jit(solution)/shard_map/pallas_call | solution.py:193
  66.2 0.1 add_add_fusion
  66.2 0.1 reshape.204
  66.3 0.6 gather_fusion.2
  67.0 0.1 reshape.198
  67.1 0.1 broadcast_select_fusion.2
  67.2 0.2 fusion.27
  67.4 0.1 copy.23
  67.5 5.8 %cholesky.44 = f32[64,64]{1,0:T(8,128)S(1)} custom-call(f32[64,64]{1,0:T(8,128)S(1)} %fusion.22), custom_call_target="Cholesky" | custom-call | tf_op jit(solution)/shard_map/jit(cholesky)/cholesky | solution.py:228
  73.3 0.6 compare_reduce_fusion.3
  74.0 0.7 fusion.11
  74.6 4.9 %custom-call.12 = f32[1,64,64]{1,2,0:T(8,128)S(1)} custom-call(f32[1,64,64]{2,1,0:T(8,128)S(1)} %fusion.11), custom_call_target="InvertDiagBlocksLowerTriangular" | custom-call | tf_op jit(solution)/shard_map/triangular_solve | solution.py:222
  79.6 0.3 fusion.4
  79.9 0.3 fusion.20
  80.2 0.2 fusion.18
  80.4 0.3 fusion.2
  80.7 0.2 fusion.38
  80.9 0.1 copy.24
  80.9 5.8 %cholesky.55 = f32[64,64]{1,0:T(8,128)S(1)} custom-call(f32[64,64]{1,0:T(8,128)S(1)} %fusion.17), custom_call_target="Cholesky" | custom-call | tf_op jit(solution)/shard_map/jit(cholesky)/cholesky | solution.py:228
  86.8 0.6 compare_reduce_fusion.2
  87.5 0.7 fusion.12
  88.1 4.9 %custom-call.13 = f32[1,64,64]{1,2,0:T(8,128)S(1)} custom-call(f32[1,64,64]{2,1,0:T(8,128)S(1)} %fusion.12), custom_call_target="InvertDiagBlocksLowerTriangular" | custom-call | tf_op jit(solution)/shard_map/triangular_solve | solution.py:222
  93.1 0.1 compare_reduce_fusion.1
  93.2 0.4 fusion.1
  93.6 0.3 fusion.39
  93.9 0.3 fusion.15
  94.1 0.2 fusion.13
  94.3 0.2 convolution_add_fusion.2
  94.6 1.1 %gather_fusion.3 = f32[128,2176]{1,0:T(8,128)S(1)} fusion(f32[256,2176]{1,0:T(8,128)S(1)} %bitcast.52, s32[1024]{0:T(1024)S(1)} %pad_clamp_fusion), kind=kCustom, calls=%fused_computation.5 | custom fusion | bytes 2228736 | tf_op jit(solution)/shard_map/jit(_take)/gather | solution.py:275
  95.6 0.0 copy-start.2
  95.6 0.1 broadcast_select_fusion
  95.8 0.1 slice_reduce_fusion
  95.9 0.2 fusion.9
  96.1 0.6 add_multiply_fusion
  96.7 0.6 copy-done.2
  97.2 3.2 %fusion = f32[256,2048]{1,0:T(8,128)} fusion(f32[256,2048]{1,0:T(8,128)S(1)} %copy-done.2, f32[128,2176]{1,0:T(8,128)S(1)} %broadcast_select_fusion, f32[256]{0:T(256)S(1)} %get-tuple-element.27, f32[256,64]{0,1:T(8,128)S(1)} %bitcast.56, f32[256,64]{0,1:T(8,128)S(1)} %convolution_add_fusion.2), kind=kOutput, calls=%fused_computation.7 | convolution fusion | flops 806387712 | bytes 5374976 | tf_op jit(solution)/shard_map/dot_general | solution.py:305
  (21 shorter events, 0.2 us)
Async XLA Ops:
  0.6 7.0 %copy-start = (s32[4096]{0:T(1024)S(1)}, s32[4096]{0:T(1024)}, u32[]{:S(2)}) copy-start(s32[4096]{0:T(1024)} %param.12) | copy-start | bytes 49156
  0.6 4.4 %copy-start.3 = (f32[256]{0:T(256)S(1)}, f32[256]{0:T(256)}, u32[]{:S(2)}) copy-start(f32[256]{0:T(256)} %param.11) | copy-start | bytes 3076
  2.6 4.9 %copy-start.5 = (s32[2,64]{1,0:T(2,128)S(1)}, s32[2,64]{1,0:T(2,128)}, u32[]{:S(2)}) copy-start(s32[2,64]{1,0:T(2,128)} %param.14) | copy-start | bytes 1540
  4.9 3.9 %copy-start.4 = (s32[4096]{0:T(1024)S(1)}, s32[4096]{0:T(1024)}, u32[]{:S(2)}) copy-start(s32[4096]{0:T(1024)} %param.13) | copy-start | bytes 49156
  9.9 1.6 %copy-start.1 = (f32[256,2048]{1,0:T(8,128)S(1)}, f32[256,2048]{1,0:T(8,128)}, u32[]{:S(2)}) copy-start(f32[256,2048]{1,0:T(8,128)} %p_ref.1) | copy-start | bytes 6291460
  95.6 1.6 %copy-start.2 = (f32[256,2048]{1,0:T(8,128)S(1)}, f32[256,2048]{1,0:T(8,128)}, u32[]{:S(2)}) copy-start(f32[256,2048]{1,0:T(8,128)} %p_ref.1) | copy-start | bytes 6291460
